TPU v7x, 512 devices: a whole 4x8x8 slice. The times are simulated.
512 devices in a mesh: ctx: 64 (over z, y_hi, core), head: 8 (over x, y_lo).
Axes of the slice: x: 4, y: 8 (y_hi: 4, y_lo: 2; y = y_hi * 2 + y_lo), z: 8, core: 2. Of those that a mesh axis runs over, the one named last changes fastest.
Arguments:
- queries: bfloat16 [65536, 4096], P(('ctx', 'head')), may hold values from -5 to 5
- keys: bfloat16 [65536, 1024], P(('ctx', 'head')), may hold values from -5 to 5
- values: bfloat16 [65536, 1024], P(('ctx', 'head')), may hold values from -5 to 5
- grad_out: bfloat16 [65536, 4096], P(('ctx', 'head')), may hold values from -5 to 5
- delta: float32 [32, 65536], P(None, ('ctx', 'head')), may hold values from -10 to 10
- doc_lengths: int32 [256], replicated, may hold values from 1 to 2048, as said below
Outputs:
- grad_queries: bfloat16 [65536, 4096], P(('ctx', 'head'))
- grad_keys: bfloat16 [65536, 1024], P(('ctx', 'head'))
- grad_values: bfloat16 [65536, 1024], P(('ctx', 'head'))
Inputs may be any that keep to these rules, and one draw needn't show every extreme that they name: `doc_lengths`: the lengths are positive and sum to 65536; no document is longer than 2048. Exactly five are 2048 long. With shards of 1024 tokens and c the shard count, they begin in the second half of shard 0, of shard c / 2 - 3, of shard c / 2 - 1, of shard c / 2 + 1, and of shard c - 3.
All inputs are finite; a program needn't handle non-finite values.
Results may differ from a plain program's by a relative error of at most 0.005.
Values may be sent and summed in bfloat16 or wider, within the bound.
A program may use at most 64 MiB of HBM per device.

v0:
```python
import jax
import jax.numpy as jnp
from jax import lax
from jax.sharding import PartitionSpec as P

HEAD_DIM = 128
QBLK = 256
KBLK = 256


NEG_FILL = -1e30


def passed_along(block, axis, distance):
    devices = range(lax.axis_size(axis))
    route = [(i - distance, i) for i in devices if i - distance in devices]
    return lax.ppermute(block, axis, route)


def doc_index(positions, doc_ends):
    return jnp.sum((doc_ends[None, :] <= positions[:, None]).astype(jnp.int32), axis=1)


def contract_first(left, right):
    return lax.dot_general(
        left, right, (((0,), (0,)), ((), ())), preferred_element_type=jnp.float32
    )


def contract_last(left, right):
    return lax.dot_general(
        left, right, (((1,), (1,)), ((), ())), preferred_element_type=jnp.float32
    )


def block_grads(
    q_rows,
    g_rows,
    d_rows,
    q_position,
    q_doc,
    first_start,
    win_keys,
    win_vals,
    win_pos,
    win_doc,
    acc_keys,
    acc_vals,
):
    n_tiles = win_keys.shape[0] // KBLK
    q_last = jnp.max(q_position)
    att_scale = HEAD_DIM ** (-0.5)
    row_count = q_rows.shape[0]

    def tile_live(tile_index):
        k_first = win_pos[0] + tile_index * KBLK
        return (k_first <= q_last) & (k_first + KBLK - 1 >= first_start)

    def tile_scores(tile_index):
        start = tile_index * KBLK
        key_tile = lax.dynamic_slice_in_dim(win_keys, start, KBLK, 0)
        k_position = lax.dynamic_slice_in_dim(win_pos, start, KBLK, 0)
        k_doc = lax.dynamic_slice_in_dim(win_doc, start, KBLK, 0)
        scores = contract_last(q_rows, key_tile) * att_scale
        allowed = (
            (k_doc[None, :] == q_doc[:, None])
            & (k_position[None, :] <= q_position[:, None])
            & (k_position[None, :] >= 0)
        )
        return (jnp.where(allowed, scores, NEG_FILL), allowed, key_tile, start)

    def stats_step(tile_index, carry):

        def stats_update(state):
            row_max, row_sum = state
            scores = tile_scores(tile_index)[0]
            new_max = jnp.maximum(row_max, jnp.max(scores, axis=1))
            row_sum = row_sum * jnp.exp(row_max - new_max) + jnp.sum(
                jnp.exp(scores - new_max[:, None]), axis=1
            )
            return (new_max, row_sum)

        return lax.cond(tile_live(tile_index), stats_update, lambda state: state, carry)

    start_stats = (
        jnp.full((row_count,), NEG_FILL, jnp.float32),
        jnp.zeros((row_count,), jnp.float32),
    )
    row_max, row_sum = lax.fori_loop(0, n_tiles, stats_step, start_stats)
    log_total = row_max + jnp.log(row_sum)

    def grad_step(tile_index, carry):

        def grad_update(state):
            dq_acc, key_acc, val_acc = state
            scores, allowed, key_tile, start = tile_scores(tile_index)
            val_tile = lax.dynamic_slice_in_dim(win_vals, start, KBLK, 0)
            probs = jnp.where(allowed, jnp.exp(scores - log_total[:, None]), 0.0)
            probs_low = probs.astype(jnp.bfloat16)
            grad_probs = contract_last(g_rows, val_tile)
            grad_scores = (probs * (grad_probs - d_rows[:, None])).astype(jnp.bfloat16)
            dq_acc = dq_acc + jnp.dot(grad_scores, key_tile, preferred_element_type=jnp.float32)
            key_part = contract_first(grad_scores, q_rows)
            val_part = contract_first(probs_low, g_rows)
            key_acc = lax.dynamic_update_slice_in_dim(
                key_acc, lax.dynamic_slice_in_dim(key_acc, start, KBLK, 0) + key_part, start, 0
            )
            val_acc = lax.dynamic_update_slice_in_dim(
                val_acc, lax.dynamic_slice_in_dim(val_acc, start, KBLK, 0) + val_part, start, 0
            )
            return (dq_acc, key_acc, val_acc)

        return lax.cond(tile_live(tile_index), grad_update, lambda state: state, carry)

    start_grads = (jnp.zeros((row_count, HEAD_DIM), jnp.float32), acc_keys, acc_vals)
    return lax.fori_loop(0, n_tiles, grad_step, start_grads)


def on_device(queries, keys, values, grad_out, delta, doc_lengths):
    q_local, k_local, v_local, g_local = (
        lax.all_to_all(queries, "head", split_axis=1, concat_axis=0, tiled=True),
        lax.all_to_all(keys, "head", split_axis=1, concat_axis=0, tiled=True),
        lax.all_to_all(values, "head", split_axis=1, concat_axis=0, tiled=True),
        lax.all_to_all(grad_out, "head", split_axis=1, concat_axis=0, tiled=True),
    )
    d_local = lax.all_to_all(delta, "head", split_axis=0, concat_axis=1, tiled=True)
    ctx_rows = q_local.shape[0]
    kv_local = k_local.shape[1] // HEAD_DIM
    heads_local = q_local.shape[1] // HEAD_DIM
    group_size = heads_local // kv_local
    near_keys, near_vals = passed_along((k_local, v_local), "ctx", 1)
    far_keys, far_vals = passed_along((k_local, v_local), "ctx", 2)
    win_keys = jnp.concatenate([far_keys, near_keys, k_local], axis=0)
    win_vals = jnp.concatenate([far_vals, near_vals, v_local], axis=0)
    base_pos = lax.axis_index("ctx") * ctx_rows
    win_pos = base_pos - 2 * ctx_rows + jnp.arange(3 * ctx_rows, dtype=jnp.int32)
    doc_ends = jnp.cumsum(doc_lengths)
    doc_starts = doc_ends - doc_lengths
    win_doc = doc_index(win_pos, doc_ends)
    q_pos_all = base_pos + jnp.arange(ctx_rows, dtype=jnp.int32)
    q_doc_all = doc_index(q_pos_all, doc_ends)
    block_count = ctx_rows // QBLK
    q_four = q_local.reshape(ctx_rows, kv_local, group_size, HEAD_DIM)
    g_four = g_local.reshape(ctx_rows, kv_local, group_size, HEAD_DIM)
    d_three = d_local.reshape(kv_local, group_size, ctx_rows)
    q_head = q_four[:, 0]
    g_head = g_four[:, 0]
    d_head = d_three[0]

    def per_block(carry, block):
        acc_keys, acc_vals = carry
        block_first = block * QBLK
        q_rows = jnp.swapaxes(lax.dynamic_slice_in_dim(q_head, block_first, QBLK, 0), 0, 1).reshape(
            group_size * QBLK, HEAD_DIM
        )
        g_rows = jnp.swapaxes(lax.dynamic_slice_in_dim(g_head, block_first, QBLK, 0), 0, 1).reshape(
            group_size * QBLK, HEAD_DIM
        )
        d_rows = lax.dynamic_slice_in_dim(d_head, block_first, QBLK, 1).reshape(group_size * QBLK)
        q_position = jnp.tile(lax.dynamic_slice_in_dim(q_pos_all, block_first, QBLK, 0), group_size)
        q_doc = jnp.tile(lax.dynamic_slice_in_dim(q_doc_all, block_first, QBLK, 0), group_size)
        q_first = base_pos + block_first
        first_start = jnp.max(jnp.where(doc_starts <= q_first, doc_starts, 0))
        dq_rows, acc_keys, acc_vals = block_grads(
            q_rows,
            g_rows,
            d_rows,
            q_position,
            q_doc,
            first_start,
            win_keys,
            win_vals,
            win_pos,
            win_doc,
            acc_keys,
            acc_vals,
        )
        return ((acc_keys, acc_vals), dq_rows)

    zero_acc = jnp.zeros((3 * ctx_rows, HEAD_DIM), jnp.float32)
    (acc_keys, acc_vals), dq_blocks = lax.scan(
        per_block, (zero_acc, zero_acc), jnp.arange(block_count, dtype=jnp.int32)
    )
    dq_blocks = dq_blocks.reshape(block_count, group_size, QBLK, HEAD_DIM).transpose(0, 2, 1, 3)
    dq_heads = dq_blocks.reshape(ctx_rows, group_size * HEAD_DIM)
    far_part_keys = acc_keys[:ctx_rows]
    far_part_vals = acc_vals[:ctx_rows]
    near_part_keys = acc_keys[ctx_rows : 2 * ctx_rows]
    near_part_vals = acc_vals[ctx_rows : 2 * ctx_rows]
    total_keys = acc_keys[2 * ctx_rows :]
    total_vals = acc_vals[2 * ctx_rows :]
    got_keys, got_vals = passed_along((near_part_keys, near_part_vals), "ctx", -1)
    far_got_keys, far_got_vals = passed_along((far_part_keys, far_part_vals), "ctx", -2)
    total_keys = total_keys + got_keys + far_got_keys
    total_vals = total_vals + got_vals + far_got_vals
    att_scale = HEAD_DIM ** (-0.5)
    dq_low = (dq_heads * att_scale).astype(jnp.bfloat16)
    dk_low = (total_keys * att_scale).astype(jnp.bfloat16)
    dv_low = total_vals.astype(jnp.bfloat16)
    grad_queries, grad_keys, grad_values = (
        lax.all_to_all(dq_low, "head", split_axis=0, concat_axis=1, tiled=True),
        lax.all_to_all(dk_low, "head", split_axis=0, concat_axis=1, tiled=True),
        lax.all_to_all(dv_low, "head", split_axis=0, concat_axis=1, tiled=True),
    )
    return (grad_queries, grad_keys, grad_values)


def solution(mesh):
    placed = (
        P(("ctx", "head"), None),
        P(("ctx", "head"), None),
        P(("ctx", "head"), None),
        P(("ctx", "head"), None),
        P(None, ("ctx", "head")),
        P(),
    )
    return jax.shard_map(
        on_device,
        mesh=mesh,
        in_specs=placed,
        out_specs=(P(("ctx", "head"), None), P(("ctx", "head"), None), P(("ctx", "head"), None)),
        check_vma=False,
    )
```

profile of v0, /device:TPU:272, one launch (start us, length us, event | category | flops | bytes accessed | tf_op | source)
XLA Modules:
  0.0 687.7 jit_solution(15009972772753179324)
XLA Ops:
  2.3 5.3 all-to-all-start.1
  9.4 5.6 all-to-all-done.1
  14.9 3.4 all-to-all-start.4
  19.7 5.9 all-to-all-done.4
  25.6 3.6 all-to-all-start
  30.5 12.2 %all-to-all-done = bf16[128,8,512]{0,2,1:T(8,128)(2,1)S(1)} async-done(((bf16[128,8,512]{0,2,1:T(8,128)(2,1)}), bf16[128,8,512]{0,2,1:T(8,128)(2,1)S(1)}, u32[]{:S(2)}, u32[]{:S(2)}) %all-to-all-start) | async-done | bytes 1048608 | tf_op jit(solution)/shard_map/all_to_all | solution.py:121
  42.6 3.6 all-to-all-start.2
  47.2 1.9 collective-permute-start.3
  49.1 4.8 collective-permute-start.2
  54.0 1.9 convert_reduce_fusion
  55.8 2.5 collective-permute-start.1
  58.4 3.6 collective-permute-start
  62.0 13.5 %collective-permute-done.3 = bf16[1024,128]{1,0:T(8,128)(2,1)S(1)} collective-permute-done((bf16[1024,128]{1,0:T(8,128)(2,1)S(1)}, bf16[1024,128]{1,0:T(8,128)(2,1)S(1)}, u32[]{:S(2)}, u32[]{:S(2)}) %collective-permute-start.3) | collective-permute-done | bytes 262176 | tf_op jit(solution)/shard_map/ppermute | solution.py:17
  75.5 4.4 collective-permute-done.2
  80.9 4.3 all-to-all-start.3
  88.7 2.3 squeeze_reshape.6
  94.3 361.7 %while.101 = (s32[]{:T(128)}, f32[3072,128]{1,0:T(8,128)}, f32[3072,128]{1,0:T(8,128)S(1)}, f32[4,1024,128]{2,1,0:T(8,128)}, s32[4]{0:T(128)S(1)}, /*index=5*/s3...) while((s32[]{:T(128)}, f32[3072,128]{1,0:T(8,128)}, ...), condition=%wide.region_17.18_spmd.clone, body=%wide.region_4.17_spmd.clone.sunk | while | flops 408363264 | bytes 13832693 | solution.py:181
  98.3 32.5 %while.102 = (s32[]{:T(128)}, f32[1024]{0:T(1024)S(1)}, f32[1024]{0:T(1024)S(1)}, s32[3072]{0:T(1024)S(1)}, s32[]{:T(128)}, /*index=5*/s32[]{:T(128)}, s32[3072]...) while((s32[]{:T(128)}, f32[1024]{0:T(1024)S(1)}, ...), condition=%wide.region_12.12_spmd.clone, body=%wide.region_7.11_spmd.clone.sunk | while | flops 69470472 | bytes 2519933 | solution.py:89
  131.1 41.1 %while.103 = (s32[]{:T(128)}, f32[1024,128]{1,0:T(8,128)S(1)}, f32[3072,128]{1,0:T(8,128)}, f32[3072,128]{1,0:T(8,128)S(1)}, s32[3072]{0:T(1024)S(1)}, /*index=5...) while((s32[]{:T(128)}, f32[1024,128]{1,0:T(8,128)S(1)}, ...), condition=%wide.region_16.16_spmd.clone, body=%wide.region_13.15_spmd.clone.sunk | while | flops 338886912 | bytes 7594989 | solution.py:116
  150.4 6.1 conditional.7
  154.7 1.8 fusion.23
  158.9 6.1 conditional.7
  163.1 1.9 fusion.23
  177.1 34.2 %while.102 = (s32[]{:T(128)}, f32[1024]{0:T(1024)S(1)}, f32[1024]{0:T(1024)S(1)}, s32[3072]{0:T(1024)S(1)}, s32[]{:T(128)}, /*index=5*/s32[]{:T(128)}, s32[3072]...) while((s32[]{:T(128)}, f32[1024]{0:T(1024)S(1)}, ...), condition=%wide.region_12.12_spmd.clone, body=%wide.region_7.11_spmd.clone.sunk | while | flops 69470472 | bytes 2519933 | solution.py:89
  211.5 47.3 %while.103 = (s32[]{:T(128)}, f32[1024,128]{1,0:T(8,128)S(1)}, f32[3072,128]{1,0:T(8,128)}, f32[3072,128]{1,0:T(8,128)S(1)}, s32[3072]{0:T(1024)S(1)}, /*index=5...) while((s32[]{:T(128)}, f32[1024,128]{1,0:T(8,128)S(1)}, ...), condition=%wide.region_16.16_spmd.clone, body=%wide.region_13.15_spmd.clone.sunk | while | flops 338886912 | bytes 7594989 | solution.py:116
  230.8 6.1 conditional.7
  235.1 1.8 fusion.23
  239.3 6.1 conditional.7
  243.6 1.9 fusion.23
  247.8 6.2 conditional.7
  252.1 1.9 fusion.23
  263.6 35.9 %while.102 = (s32[]{:T(128)}, f32[1024]{0:T(1024)S(1)}, f32[1024]{0:T(1024)S(1)}, s32[3072]{0:T(1024)S(1)}, s32[]{:T(128)}, /*index=5*/s32[]{:T(128)}, s32[3072]...) while((s32[]{:T(128)}, f32[1024]{0:T(1024)S(1)}, ...), condition=%wide.region_12.12_spmd.clone, body=%wide.region_7.11_spmd.clone.sunk | while | flops 69470472 | bytes 2519933 | solution.py:89
  299.7 53.3 %while.103 = (s32[]{:T(128)}, f32[1024,128]{1,0:T(8,128)S(1)}, f32[3072,128]{1,0:T(8,128)}, f32[3072,128]{1,0:T(8,128)S(1)}, s32[3072]{0:T(1024)S(1)}, /*index=5...) while((s32[]{:T(128)}, f32[1024,128]{1,0:T(8,128)S(1)}, ...), condition=%wide.region_16.16_spmd.clone, body=%wide.region_13.15_spmd.clone.sunk | while | flops 338886912 | bytes 7594989 | solution.py:116
  319.0 6.1 conditional.7
  323.3 1.8 fusion.23
  327.5 6.1 conditional.7
  331.8 1.9 fusion.23
  336.0 6.1 conditional.7
  340.3 1.9 fusion.23
  344.5 6.1 conditional.7
  348.8 1.9 fusion.23
  357.9 37.6 %while.102 = (s32[]{:T(128)}, f32[1024]{0:T(1024)S(1)}, f32[1024]{0:T(1024)S(1)}, s32[3072]{0:T(1024)S(1)}, s32[]{:T(128)}, /*index=5*/s32[]{:T(128)}, s32[3072]...) while((s32[]{:T(128)}, f32[1024]{0:T(1024)S(1)}, ...), condition=%wide.region_12.12_spmd.clone, body=%wide.region_7.11_spmd.clone.sunk | while | flops 69470472 | bytes 2519933 | solution.py:89
  395.7 59.5 %while.103 = (s32[]{:T(128)}, f32[1024,128]{1,0:T(8,128)S(1)}, f32[3072,128]{1,0:T(8,128)}, f32[3072,128]{1,0:T(8,128)S(1)}, s32[3072]{0:T(1024)S(1)}, /*index=5...) while((s32[]{:T(128)}, f32[1024,128]{1,0:T(8,128)S(1)}, ...), condition=%wide.region_16.16_spmd.clone, body=%wide.region_13.15_spmd.clone.sunk | while | flops 338886912 | bytes 7594989 | solution.py:116
  415.0 6.1 conditional.7
  423.5 6.1 conditional.7
  427.8 1.9 fusion.23
  432.0 6.1 conditional.7
  436.3 1.9 fusion.23
  440.5 6.1 conditional.7
  444.8 1.9 fusion.23
  449.1 6.1 conditional.7
  453.3 1.9 fusion.23
  457.3 100.3 %collective-permute-start.4 = (f32[1024,128]{1,0:T(8,128)S(1)}, f32[1024,128]{1,0:T(8,128)S(1)}, u32[]{:S(2)}, u32[]{:S(2)}) collective-permute-start(f32[1024,128]{1,0:T(8,128)S(1)} %get-tuple-element.1695), channel_id=1, source_target_pairs={{8,0},{16,8},{24,16},{32,24},{40,32},{48,40},{56,48},{64,56},{72,6... | collective-permute-start | bytes 1572872 | tf_op jit(solution)/shard_map/ppermute | solution.py:17
  557.6 4.1 collective-permute-start.5
  562.7 1.9 collective-permute-start.6
  564.7 1.9 collective-permute-start.7
  566.6 21.5 %collective-permute-done.4 = f32[1024,128]{1,0:T(8,128)S(1)} collective-permute-done((f32[1024,128]{1,0:T(8,128)S(1)}, f32[1024,128]{1,0:T(8,128)S(1)}, u32[]{:S(2)}, u32[]{:S(2)}) %collective-permute-start.4) | collective-permute-done | bytes 524320 | tf_op jit(solution)/shard_map/ppermute | solution.py:17
  588.0 37.2 %collective-permute-done.5 = f32[1024,128]{1,0:T(8,128)S(1)} collective-permute-done((f32[1024,128]{1,0:T(8,128)S(1)}, f32[1024,128]{1,0:T(8,128)S(1)}, u32[]{:S(2)}, u32[]{:S(2)}) %collective-permute-start.5) | collective-permute-done | bytes 524320 | tf_op jit(solution)/shard_map/ppermute | solution.py:17
  627.1 13.7 %all-to-all-start.6 = ((bf16[8,128,128]{2,1,0:T(8,128)(2,1)}), bf16[8,128,128]{2,1,0:T(8,128)(2,1)S(1)}, u32[]{:S(2)}, u32[]{:S(2)}) async-start(bf16[8,128,128]{2,1,0:T(8,128)(2,1)} %bitcast.22), calls=%async_computation.6 | async-start | bytes 524288 | tf_op jit(solution)/shard_map/all_to_all | solution.py:202
  640.7 17.6 %collective-permute-done.7 = f32[1024,128]{1,0:T(8,128)S(1)} collective-permute-done((f32[1024,128]{1,0:T(8,128)}, f32[1024,128]{1,0:T(8,128)S(1)}, u32[]{:S(2)}, u32[]{:S(2)}) %collective-permute-start.7) | collective-permute-done | bytes 524320 | tf_op jit(solution)/shard_map/ppermute | solution.py:17
  659.1 4.2 all-to-all-start.7
  667.3 3.4 all-to-all-done.7
  670.7 3.6 all-to-all-start.5
  676.3 9.4 %all-to-all-done.5 = bf16[8,128,512]{2,1,0:T(8,128)(2,1)S(1)} async-done(((bf16[8,128,512]{2,1,0:T(8,128)(2,1)}), bf16[8,128,512]{2,1,0:T(8,128)(2,1)S(1)}, u32[]{:S(2)}, u32[]{:S(2)}) %all-to-all-start.5) | async-done | bytes 1048608 | tf_op jit(solution)/shard_map/all_to_all | solution.py:201
  (567 shorter events, 206.5 us)
Async XLA Ops:
  0.6 1.0 copy-start
  0.6 17.7 %copy-start.1 = (bf16[128,4096]{1,0:T(8,128)(2,1)S(1)}, bf16[128,4096]{1,0:T(8,128)(2,1)}, u32[]{:S(2)}) copy-start(bf16[128,4096]{1,0:T(8,128)(2,1)} %param.16) | copy-start | bytes 3145732
  2.3 12.6 %all-to-all-start.1 = ((bf16[128,8,128]{2,0,1:T(8,128)(2,1)}), bf16[128,8,128]{2,0,1:T(8,128)(2,1)S(1)}, u32[]{:S(2)}, u32[]{:S(2)}) async-start(bf16[128,8,128]{2,0,1:T(8,128)(2,1)} %copy_bitcast_fusion.2), calls=%async_computation.1 | async-start | bytes 524288 | tf_op jit(solution)/shard_map/all_to_all | solution.py:122
  14.9 10.6 %all-to-all-start.4 = ((bf16[128,8,128]{2,0,1:T(8,128)(2,1)}), bf16[128,8,128]{2,0,1:T(8,128)(2,1)S(1)}, u32[]{:S(2)}, u32[]{:S(2)}) async-start(bf16[128,8,128]{2,0,1:T(8,128)(2,1)} %copy_bitcast_fusion.1), calls=%async_computation.4 | async-start | bytes 524288 | tf_op jit(solution)/shard_map/all_to_all | solution.py:123
  19.7 9.5 %copy-start.2 = (bf16[128,4096]{1,0:T(8,128)(2,1)S(1)}, bf16[128,4096]{1,0:T(8,128)(2,1)}, u32[]{:S(2)}) copy-start(bf16[128,4096]{1,0:T(8,128)(2,1)} %param.19) | copy-start | bytes 3145732
  25.6 17.0 %all-to-all-start = ((bf16[128,8,512]{0,2,1:T(8,128)(2,1)}), bf16[128,8,512]{0,2,1:T(8,128)(2,1)S(1)}, u32[]{:S(2)}, u32[]{:S(2)}) async-start(bf16[128,8,512]{0,2,1:T(8,128)(2,1)} %bitcast.5), calls=%async_computation | async-start | bytes 2097152 | tf_op jit(solution)/shard_map/all_to_all | solution.py:121
  30.5 15.7 %copy-start.3 = (s32[256]{0:T(256)S(1)}, s32[256]{0:T(256)}, u32[]{:S(2)}) copy-start(s32[256]{0:T(256)} %param.21) | copy-start | bytes 3076
  42.6 38.2 %all-to-all-start.2 = ((bf16[128,8,512]{0,2,1:T(8,128)(2,1)}), bf16[128,8,512]{0,2,1:T(8,128)(2,1)S(1)}, u32[]{:S(2)}, u32[]{:S(2)}) async-start(bf16[128,8,512]{0,2,1:T(8,128)(2,1)} %bitcast.116), calls=%async_computation.2 | async-start | bytes 2097152 | tf_op jit(solution)/shard_map/all_to_all | solution.py:124
  47.2 28.3 %collective-permute-start.3 = (bf16[1024,128]{1,0:T(8,128)(2,1)S(1)}, bf16[1024,128]{1,0:T(8,128)(2,1)S(1)}, u32[]{:S(2)}, u32[]{:S(2)}) collective-permute-start(bf16[1024,128]{1,0:T(8,128)(2,1)S(1)} %bitcast.130), channel_id=1, source_target_pairs={{0,8},{8,16},{16,24},{24,32},{32,40},{40,48},{48,56},{56,64},{64,7... | collective-permute-start | bytes 786440 | tf_op jit(solution)/shard_map/ppermute | solution.py:17
  49.1 30.8 %collective-permute-start.2 = (bf16[1024,128]{1,0:T(8,128)(2,1)S(1)}, bf16[1024,128]{1,0:T(8,128)(2,1)S(1)}, u32[]{:S(2)}, u32[]{:S(2)}) collective-permute-start(bf16[1024,128]{1,0:T(8,128)(2,1)S(1)} %bitcast.131), channel_id=1, source_target_pairs={{0,16},{8,24},{16,32},{24,40},{32,48},{40,56},{48,64},{56,72},{64,... | collective-permute-start | bytes 786440 | tf_op jit(solution)/shard_map/ppermute | solution.py:17
  55.8 30.3 %collective-permute-start.1 = (bf16[1024,128]{1,0:T(8,128)(2,1)S(1)}, bf16[1024,128]{1,0:T(8,128)(2,1)S(1)}, u32[]{:S(2)}, u32[]{:S(2)}) collective-permute-start(bf16[1024,128]{1,0:T(8,128)(2,1)S(1)} %bitcast.127), channel_id=1, source_target_pairs={{0,8},{8,16},{16,24},{24,32},{32,40},{40,48},{48,56},{56,64},{64,7... | collective-permute-start | bytes 786440 | tf_op jit(solution)/shard_map/ppermute | solution.py:17
  58.4 27.8 %collective-permute-start = (bf16[1024,128]{1,0:T(8,128)(2,1)S(1)}, bf16[1024,128]{1,0:T(8,128)(2,1)S(1)}, u32[]{:S(2)}, u32[]{:S(2)}) collective-permute-start(bf16[1024,128]{1,0:T(8,128)(2,1)S(1)} %bitcast.128), channel_id=1, source_target_pairs={{0,16},{8,24},{16,32},{24,40},{32,48},{40,56},{48,64},{56,72},{64,... | collective-permute-start | bytes 786440 | tf_op jit(solution)/shard_map/ppermute | solution.py:17
  80.9 12.1 %all-to-all-start.3 = ((f32[8,4,128]{2,1,0:T(4,128)}), f32[8,4,128]{2,1,0:T(4,128)S(1)}, u32[]{:S(2)}, u32[]{:S(2)}) async-start(f32[8,4,128]{2,1,0:T(4,128)} %bitcast.12), calls=%async_computation.3 | async-start | bytes 32768 | tf_op jit(solution)/shard_map/all_to_all | solution.py:126
  457.3 130.7 %collective-permute-start.4 = (f32[1024,128]{1,0:T(8,128)S(1)}, f32[1024,128]{1,0:T(8,128)S(1)}, u32[]{:S(2)}, u32[]{:S(2)}) collective-permute-start(f32[1024,128]{1,0:T(8,128)S(1)} %get-tuple-element.1695), channel_id=1, source_target_pairs={{8,0},{16,8},{24,16},{32,24},{40,32},{48,40},{56,48},{64,56},{72,6... | collective-permute-start | bytes 1572872 | tf_op jit(solution)/shard_map/ppermute | solution.py:17
  557.6 67.6 %collective-permute-start.5 = (f32[1024,128]{1,0:T(8,128)S(1)}, f32[1024,128]{1,0:T(8,128)S(1)}, u32[]{:S(2)}, u32[]{:S(2)}) collective-permute-start(f32[1024,128]{1,0:T(8,128)S(1)} %get-tuple-element.1696), channel_id=1, source_target_pairs={{16,0},{24,8},{32,16},{40,24},{48,32},{56,40},{64,48},{72,56},{80,... | collective-permute-start | bytes 1572872 | tf_op jit(solution)/shard_map/ppermute | solution.py:17
  562.7 78.0 %collective-permute-start.6 = (f32[1024,128]{1,0:T(8,128)}, f32[1024,128]{1,0:T(8,128)S(1)}, u32[]{:S(2)}, u32[]{:S(2)}) collective-permute-start(f32[1024,128]{1,0:T(8,128)} %get-tuple-element.1693), channel_id=1, source_target_pairs={{8,0},{16,8},{24,16},{32,24},{40,32},{48,40},{56,48},{64,56},{72,6... | collective-permute-start | bytes 1572872 | tf_op jit(solution)/shard_map/ppermute | solution.py:17
  564.7 93.7 %collective-permute-start.7 = (f32[1024,128]{1,0:T(8,128)}, f32[1024,128]{1,0:T(8,128)S(1)}, u32[]{:S(2)}, u32[]{:S(2)}) collective-permute-start(f32[1024,128]{1,0:T(8,128)} %get-tuple-element.1694), channel_id=1, source_target_pairs={{16,0},{24,8},{32,16},{40,24},{48,32},{56,40},{64,48},{72,56},{80,... | collective-permute-start | bytes 1572872 | tf_op jit(solution)/shard_map/ppermute | solution.py:17
  627.1 32.1 %all-to-all-start.6 = ((bf16[8,128,128]{2,1,0:T(8,128)(2,1)}), bf16[8,128,128]{2,1,0:T(8,128)(2,1)S(1)}, u32[]{:S(2)}, u32[]{:S(2)}) async-start(bf16[8,128,128]{2,1,0:T(8,128)(2,1)} %bitcast.22), calls=%async_computation.6 | async-start | bytes 524288 | tf_op jit(solution)/shard_map/all_to_all | solution.py:202
  659.1 11.5 %all-to-all-start.7 = ((bf16[8,128,128]{2,1,0:T(8,128)(2,1)}), bf16[8,128,128]{2,1,0:T(8,128)(2,1)S(1)}, u32[]{:S(2)}, u32[]{:S(2)}) async-start(bf16[8,128,128]{2,1,0:T(8,128)(2,1)} %bitcast.25), calls=%async_computation.7 | async-start | bytes 524288 | tf_op jit(solution)/shard_map/all_to_all | solution.py:203
  670.7 15.0 %all-to-all-start.5 = ((bf16[8,128,512]{2,1,0:T(8,128)(2,1)}), bf16[8,128,512]{2,1,0:T(8,128)(2,1)S(1)}, u32[]{:S(2)}, u32[]{:S(2)}) async-start(bf16[8,128,512]{2,1,0:T(8,128)(2,1)} %convert_element_type.58), calls=%async_computation.5 | async-start | bytes 2097152 | tf_op jit(solution)/shard_map/all_to_all | solution.py:201
where the time goes:
time: 697 us; the launch traced here: 688 us
  loops' own time  183 us (26%)
  starting transfers between devices  163 us (23%)
  waiting for transfers between devices  132 us (19%)
  matrix products  101 us (14%)
  local copies, waits for them, and re-layouts  89.3 us (13%)
  other arithmetic  19 us (3%)
    ppermute x8, starting transfers between devices, passed_along(): return lax.ppermute(block, axis, route)  121 us
    ppermute x8, waiting for transfers between devices, passed_along(): return lax.ppermute(block, axis, route)  95.2 us
    another operation x4, loops' own time, block_grads(): return lax.fori_loop(0, n_tiles, grad_step, start_grads)  89.2 us
    another operation x4, loops' own time, block_grads(): row_max, row_sum = lax.fori_loop(0, n_tiles, stats_step, start_stats)  89.1 us
    dot_general x42, matrix products, contract_last(): lax.dot_general(left, right, (((1,), (1,)), ((), ())), preferred_element_...  53.8 us
    slice x96, local copies, waits for them, and re-layouts, tile_live(): k_first = win_pos[0] + tile_index * KBLK  52.6 us
    dot_general x28, matrix products, contract_first(): lax.dot_general(left, right, (((0,), (0,)), ((), ())), preferred_element_...  30.2 us
    dot_general x14, matrix products, grad_update(): jnp.dot(grad_scores, key_tile, preferred_element_type=jnp.float32)  16.9 us
  transfers between devices with their start and end apart: 16, of which 11 were waited for; matrix products, arithmetic and copies ran while one was open for 4% of the time, Pallas kernels for 0%

commit v1 on v0

--- a/solution.py
+++ b/solution.py
@@ -134,7 +134,8 @@
     win_vals = jnp.concatenate([far_vals, near_vals, v_local], axis=0)
     base_pos = lax.axis_index("ctx") * ctx_rows
     win_pos = base_pos - 2 * ctx_rows + jnp.arange(3 * ctx_rows, dtype=jnp.int32)
-    doc_ends = jnp.cumsum(doc_lengths)
+    slots = jnp.arange(doc_lengths.shape[0], dtype=jnp.int32)
+    doc_ends = jnp.sum(jnp.where(slots[:, None] <= slots[None, :], doc_lengths[:, None], 0), axis=0)
     doc_starts = doc_ends - doc_lengths
     win_doc = doc_index(win_pos, doc_ends)
     q_pos_all = base_pos + jnp.arange(ctx_rows, dtype=jnp.int32)

time: 697 us -> 707 us (1.014)
  loops' own time: 183 us -> 195 us
  transfers between devices with their start and end apart: 16 -> 16, of which waited for: 11 -> 11; matrix products, arithmetic and copies ran while one was open for 4% -> 3% of each run, Pallas kernels for 0% -> 0%
where the time goes in v1:
time: 707 us; the launch traced here: 698 us
  loops' own time  195 us (28%)
  starting transfers between devices  162 us (23%)
  waiting for transfers between devices  132 us (19%)
  matrix products  101 us (14%)
  local copies, waits for them, and re-layouts  87.8 us (12%)
  other arithmetic  19.1 us (3%)
    ppermute x8, starting transfers between devices, passed_along(): return lax.ppermute(block, axis, route)  121 us
    ppermute x8, waiting for transfers between devices, passed_along(): return lax.ppermute(block, axis, route)  95.4 us
    another operation x4, loops' own time, block_grads(): return lax.fori_loop(0, n_tiles, grad_step, start_grads)  94.7 us
    another operation x4, loops' own time, block_grads(): row_max, row_sum = lax.fori_loop(0, n_tiles, stats_step, start_stats)  94.6 us
    dot_general x42, matrix products, contract_last(): lax.dot_general(left, right, (((1,), (1,)), ((), ())), preferred_element_...  53.9 us
    slice x96, local copies, waits for them, and re-layouts, tile_live(): k_first = win_pos[0] + tile_index * KBLK  51.3 us
    dot_general x28, matrix products, contract_first(): lax.dot_general(left, right, (((0,), (0,)), ((), ())), preferred_element_...  30.3 us
    dot_general x14, matrix products, grad_update(): jnp.dot(grad_scores, key_tile, preferred_element_type=jnp.float32)  16.9 us
  transfers between devices with their start and end apart: 16, of which 11 were waited for; matrix products, arithmetic and copies ran while one was open for 3% of the time, Pallas kernels for 0%

profile of v1, /device:TPU:272, one launch (start us, length us, event | category | flops | bytes accessed | tf_op | source)
XLA Modules:
  0.0 697.6 jit_solution(3326054109589514134)
XLA Ops:
  2.3 5.3 all-to-all-start.1
  9.4 5.6 all-to-all-done.1
  14.9 3.4 all-to-all-start.4
  19.7 5.9 all-to-all-done.4
  25.6 3.6 all-to-all-start
  30.5 12.2 %all-to-all-done = bf16[128,8,512]{0,2,1:T(8,128)(2,1)S(1)} async-done(((bf16[128,8,512]{0,2,1:T(8,128)(2,1)}), bf16[128,8,512]{0,2,1:T(8,128)(2,1)S(1)}, u32[]{:S(2)}, u32[]{:S(2)}) %all-to-all-start) | async-done | bytes 1048608 | tf_op jit(solution)/shard_map/all_to_all | solution.py:121
  42.6 3.6 all-to-all-start.2
  46.7 1.9 collective-permute-start.3
  48.6 4.8 collective-permute-start.2
  53.5 1.9 convert_reduce_fusion
  55.4 2.5 collective-permute-start.1
  57.9 3.6 collective-permute-start
  61.5 13.5 %collective-permute-done.3 = bf16[1024,128]{1,0:T(8,128)(2,1)S(1)} collective-permute-done((bf16[1024,128]{1,0:T(8,128)(2,1)S(1)}, bf16[1024,128]{1,0:T(8,128)(2,1)S(1)}, u32[]{:S(2)}, u32[]{:S(2)}) %collective-permute-start.3) | collective-permute-done | bytes 262176 | tf_op jit(solution)/shard_map/ppermute | solution.py:17
  75.0 5.3 collective-permute-done.2
  81.3 4.3 all-to-all-start.3
  88.7 2.3 squeeze_reshape.6
  94.3 372.0 %while.101 = (s32[]{:T(128)}, f32[3072,128]{1,0:T(8,128)}, f32[3072,128]{1,0:T(8,128)S(1)}, f32[4,1024,128]{2,1,0:T(8,128)}, s32[4]{0:T(128)S(1)}, /*index=5*/s3...) while((s32[]{:T(128)}, f32[3072,128]{1,0:T(8,128)}, ...), condition=%wide.region_16.17_spmd.clone, body=%wide.region_3.16_spmd.clone.sunk | while | flops 408363264 | bytes 13832693 | solution.py:182
  98.4 33.4 %while.102 = (s32[]{:T(128)}, f32[1024]{0:T(1024)S(1)}, f32[1024]{0:T(1024)S(1)}, s32[3072]{0:T(1024)S(1)}, s32[]{:T(128)}, /*index=5*/s32[]{:T(128)}, s32[3072]...) while((s32[]{:T(128)}, f32[1024]{0:T(1024)S(1)}, ...), condition=%wide.region_11.11_spmd.clone, body=%wide.region_6.10_spmd.clone.sunk | while | flops 69470472 | bytes 2519933 | solution.py:89
  132.1 42.7 %while.103 = (s32[]{:T(128)}, f32[1024,128]{1,0:T(8,128)S(1)}, f32[3072,128]{1,0:T(8,128)}, f32[3072,128]{1,0:T(8,128)S(1)}, s32[3072]{0:T(1024)S(1)}, /*index=5...) while((s32[]{:T(128)}, f32[1024,128]{1,0:T(8,128)S(1)}, ...), condition=%wide.region_15.15_spmd.clone, body=%wide.region_12.14_spmd.clone.sunk | while | flops 338886912 | bytes 7594989 | solution.py:116
  152.4 6.2 conditional.7
  156.7 1.9 fusion.23
  161.1 6.1 conditional.7
  165.3 1.9 fusion.23
  179.7 35.1 %while.102 = (s32[]{:T(128)}, f32[1024]{0:T(1024)S(1)}, f32[1024]{0:T(1024)S(1)}, s32[3072]{0:T(1024)S(1)}, s32[]{:T(128)}, /*index=5*/s32[]{:T(128)}, s32[3072]...) while((s32[]{:T(128)}, f32[1024]{0:T(1024)S(1)}, ...), condition=%wide.region_11.11_spmd.clone, body=%wide.region_6.10_spmd.clone.sunk | while | flops 69470472 | bytes 2519933 | solution.py:89
  215.1 48.8 %while.103 = (s32[]{:T(128)}, f32[1024,128]{1,0:T(8,128)S(1)}, f32[3072,128]{1,0:T(8,128)}, f32[3072,128]{1,0:T(8,128)S(1)}, s32[3072]{0:T(1024)S(1)}, /*index=5...) while((s32[]{:T(128)}, f32[1024,128]{1,0:T(8,128)S(1)}, ...), condition=%wide.region_15.15_spmd.clone, body=%wide.region_12.14_spmd.clone.sunk | while | flops 338886912 | bytes 7594989 | solution.py:116
  235.4 6.2 conditional.7
  239.7 1.9 fusion.23
  244.1 6.1 conditional.7
  248.3 1.9 fusion.23
  252.7 6.1 conditional.7
  257.0 1.9 fusion.23
  268.9 36.8 %while.102 = (s32[]{:T(128)}, f32[1024]{0:T(1024)S(1)}, f32[1024]{0:T(1024)S(1)}, s32[3072]{0:T(1024)S(1)}, s32[]{:T(128)}, /*index=5*/s32[]{:T(128)}, s32[3072]...) while((s32[]{:T(128)}, f32[1024]{0:T(1024)S(1)}, ...), condition=%wide.region_11.11_spmd.clone, body=%wide.region_6.10_spmd.clone.sunk | while | flops 69470472 | bytes 2519933 | solution.py:89
  305.9 54.9 %while.103 = (s32[]{:T(128)}, f32[1024,128]{1,0:T(8,128)S(1)}, f32[3072,128]{1,0:T(8,128)}, f32[3072,128]{1,0:T(8,128)S(1)}, s32[3072]{0:T(1024)S(1)}, /*index=5...) while((s32[]{:T(128)}, f32[1024,128]{1,0:T(8,128)S(1)}, ...), condition=%wide.region_15.15_spmd.clone, body=%wide.region_12.14_spmd.clone.sunk | while | flops 338886912 | bytes 7594989 | solution.py:116
  326.2 6.2 conditional.7
  330.5 1.9 fusion.23
  334.9 6.2 conditional.7
  339.2 1.9 fusion.23
  343.5 6.1 conditional.7
  347.8 1.9 fusion.23
  352.2 6.1 conditional.7
  365.8 38.5 %while.102 = (s32[]{:T(128)}, f32[1024]{0:T(1024)S(1)}, f32[1024]{0:T(1024)S(1)}, s32[3072]{0:T(1024)S(1)}, s32[]{:T(128)}, /*index=5*/s32[]{:T(128)}, s32[3072]...) while((s32[]{:T(128)}, f32[1024]{0:T(1024)S(1)}, ...), condition=%wide.region_11.11_spmd.clone, body=%wide.region_6.10_spmd.clone.sunk | while | flops 69470472 | bytes 2519933 | solution.py:89
  404.5 61.0 %while.103 = (s32[]{:T(128)}, f32[1024,128]{1,0:T(8,128)S(1)}, f32[3072,128]{1,0:T(8,128)}, f32[3072,128]{1,0:T(8,128)S(1)}, s32[3072]{0:T(1024)S(1)}, /*index=5...) while((s32[]{:T(128)}, f32[1024,128]{1,0:T(8,128)S(1)}, ...), condition=%wide.region_15.15_spmd.clone, body=%wide.region_12.14_spmd.clone.sunk | while | flops 338886912 | bytes 7594989 | solution.py:116
  424.8 6.2 conditional.7
  429.1 1.9 fusion.23
  433.5 6.2 conditional.7
  437.8 1.9 fusion.23
  442.1 6.1 conditional.7
  446.4 1.9 fusion.23
  450.8 6.1 conditional.7
  455.1 1.8 fusion.23
  459.4 6.1 conditional.7
  463.7 1.9 fusion.23
  467.7 100.2 %collective-permute-start.4 = (f32[1024,128]{1,0:T(8,128)S(1)}, f32[1024,128]{1,0:T(8,128)S(1)}, u32[]{:S(2)}, u32[]{:S(2)}) collective-permute-start(f32[1024,128]{1,0:T(8,128)S(1)} %get-tuple-element.1693), channel_id=1, source_target_pairs={{8,0},{16,8},{24,16},{32,24},{40,32},{48,40},{56,48},{64,56},{72,6... | collective-permute-start | bytes 1572872 | tf_op jit(solution)/shard_map/ppermute | solution.py:17
  567.8 4.1 collective-permute-start.5
  572.9 1.9 collective-permute-start.6
  574.8 1.9 collective-permute-start.7
  576.8 21.6 %collective-permute-done.4 = f32[1024,128]{1,0:T(8,128)S(1)} collective-permute-done((f32[1024,128]{1,0:T(8,128)S(1)}, f32[1024,128]{1,0:T(8,128)S(1)}, u32[]{:S(2)}, u32[]{:S(2)}) %collective-permute-start.4) | collective-permute-done | bytes 524320 | tf_op jit(solution)/shard_map/ppermute | solution.py:17
  598.4 36.7 %collective-permute-done.5 = f32[1024,128]{1,0:T(8,128)S(1)} collective-permute-done((f32[1024,128]{1,0:T(8,128)S(1)}, f32[1024,128]{1,0:T(8,128)S(1)}, u32[]{:S(2)}, u32[]{:S(2)}) %collective-permute-start.5) | collective-permute-done | bytes 524320 | tf_op jit(solution)/shard_map/ppermute | solution.py:17
  636.9 13.6 %all-to-all-start.6 = ((bf16[8,128,128]{2,1,0:T(8,128)(2,1)}), bf16[8,128,128]{2,1,0:T(8,128)(2,1)S(1)}, u32[]{:S(2)}, u32[]{:S(2)}) async-start(bf16[8,128,128]{2,1,0:T(8,128)(2,1)} %bitcast.20), calls=%async_computation.6 | async-start | bytes 524288 | tf_op jit(solution)/shard_map/all_to_all | solution.py:203
  650.6 17.6 %collective-permute-done.7 = f32[1024,128]{1,0:T(8,128)S(1)} collective-permute-done((f32[1024,128]{1,0:T(8,128)}, f32[1024,128]{1,0:T(8,128)S(1)}, u32[]{:S(2)}, u32[]{:S(2)}) %collective-permute-start.7) | collective-permute-done | bytes 524320 | tf_op jit(solution)/shard_map/ppermute | solution.py:17
  669.0 4.2 all-to-all-start.7
  677.1 3.4 all-to-all-done.7
  680.6 3.6 all-to-all-start.5
  686.2 9.4 %all-to-all-done.5 = bf16[8,128,512]{2,1,0:T(8,128)(2,1)S(1)} async-done(((bf16[8,128,512]{2,1,0:T(8,128)(2,1)}), bf16[8,128,512]{2,1,0:T(8,128)(2,1)S(1)}, u32[]{:S(2)}, u32[]{:S(2)}) %all-to-all-start.5) | async-done | bytes 1048608 | tf_op jit(solution)/shard_map/all_to_all | solution.py:202
  (564 shorter events, 204.6 us)
Async XLA Ops:
  0.6 1.0 copy-start
  0.6 17.7 %copy-start.1 = (bf16[128,4096]{1,0:T(8,128)(2,1)S(1)}, bf16[128,4096]{1,0:T(8,128)(2,1)}, u32[]{:S(2)}) copy-start(bf16[128,4096]{1,0:T(8,128)(2,1)} %param.16) | copy-start | bytes 3145732
  2.3 12.6 %all-to-all-start.1 = ((bf16[128,8,128]{2,0,1:T(8,128)(2,1)}), bf16[128,8,128]{2,0,1:T(8,128)(2,1)S(1)}, u32[]{:S(2)}, u32[]{:S(2)}) async-start(bf16[128,8,128]{2,0,1:T(8,128)(2,1)} %copy_bitcast_fusion.2), calls=%async_computation.1 | async-start | bytes 524288 | tf_op jit(solution)/shard_map/all_to_all | solution.py:122
  14.9 10.6 %all-to-all-start.4 = ((bf16[128,8,128]{2,0,1:T(8,128)(2,1)}), bf16[128,8,128]{2,0,1:T(8,128)(2,1)S(1)}, u32[]{:S(2)}, u32[]{:S(2)}) async-start(bf16[128,8,128]{2,0,1:T(8,128)(2,1)} %copy_bitcast_fusion.1), calls=%async_computation.4 | async-start | bytes 524288 | tf_op jit(solution)/shard_map/all_to_all | solution.py:123
  19.7 9.5 %copy-start.2 = (bf16[128,4096]{1,0:T(8,128)(2,1)S(1)}, bf16[128,4096]{1,0:T(8,128)(2,1)}, u32[]{:S(2)}) copy-start(bf16[128,4096]{1,0:T(8,128)(2,1)} %param.19) | copy-start | bytes 3145732
  25.6 17.0 %all-to-all-start = ((bf16[128,8,512]{0,2,1:T(8,128)(2,1)}), bf16[128,8,512]{0,2,1:T(8,128)(2,1)S(1)}, u32[]{:S(2)}, u32[]{:S(2)}) async-start(bf16[128,8,512]{0,2,1:T(8,128)(2,1)} %bitcast.3), calls=%async_computation | async-start | bytes 2097152 | tf_op jit(solution)/shard_map/all_to_all | solution.py:121
  30.5 15.7 %copy-start.3 = (s32[256]{0:T(256)S(1)}, s32[256]{0:T(256)}, u32[]{:S(2)}) copy-start(s32[256]{0:T(256)} %param.21) | copy-start | bytes 3076
  42.6 38.7 %all-to-all-start.2 = ((bf16[128,8,512]{0,2,1:T(8,128)(2,1)}), bf16[128,8,512]{0,2,1:T(8,128)(2,1)S(1)}, u32[]{:S(2)}, u32[]{:S(2)}) async-start(bf16[128,8,512]{0,2,1:T(8,128)(2,1)} %bitcast.112), calls=%async_computation.2 | async-start | bytes 2097152 | tf_op jit(solution)/shard_map/all_to_all | solution.py:124
  46.7 28.3 %collective-permute-start.3 = (bf16[1024,128]{1,0:T(8,128)(2,1)S(1)}, bf16[1024,128]{1,0:T(8,128)(2,1)S(1)}, u32[]{:S(2)}, u32[]{:S(2)}) collective-permute-start(bf16[1024,128]{1,0:T(8,128)(2,1)S(1)} %bitcast.126), channel_id=1, source_target_pairs={{0,8},{8,16},{16,24},{24,32},{32,40},{40,48},{48,56},{56,64},{64,7... | collective-permute-start | bytes 786440 | tf_op jit(solution)/shard_map/ppermute | solution.py:17
  48.6 31.7 %collective-permute-start.2 = (bf16[1024,128]{1,0:T(8,128)(2,1)S(1)}, bf16[1024,128]{1,0:T(8,128)(2,1)S(1)}, u32[]{:S(2)}, u32[]{:S(2)}) collective-permute-start(bf16[1024,128]{1,0:T(8,128)(2,1)S(1)} %bitcast.127), channel_id=1, source_target_pairs={{0,16},{8,24},{16,32},{24,40},{32,48},{40,56},{48,64},{56,72},{64,... | collective-permute-start | bytes 786440 | tf_op jit(solution)/shard_map/ppermute | solution.py:17
  55.4 30.8 %collective-permute-start.1 = (bf16[1024,128]{1,0:T(8,128)(2,1)S(1)}, bf16[1024,128]{1,0:T(8,128)(2,1)S(1)}, u32[]{:S(2)}, u32[]{:S(2)}) collective-permute-start(bf16[1024,128]{1,0:T(8,128)(2,1)S(1)} %bitcast.123), channel_id=1, source_target_pairs={{0,8},{8,16},{16,24},{24,32},{32,40},{40,48},{48,56},{56,64},{64,7... | collective-permute-start | bytes 786440 | tf_op jit(solution)/shard_map/ppermute | solution.py:17
  57.9 28.3 %collective-permute-start = (bf16[1024,128]{1,0:T(8,128)(2,1)S(1)}, bf16[1024,128]{1,0:T(8,128)(2,1)S(1)}, u32[]{:S(2)}, u32[]{:S(2)}) collective-permute-start(bf16[1024,128]{1,0:T(8,128)(2,1)S(1)} %bitcast.124), channel_id=1, source_target_pairs={{0,16},{8,24},{16,32},{24,40},{32,48},{40,56},{48,64},{56,72},{64,... | collective-permute-start | bytes 786440 | tf_op jit(solution)/shard_map/ppermute | solution.py:17
  81.3 11.7 %all-to-all-start.3 = ((f32[8,4,128]{2,1,0:T(4,128)}), f32[8,4,128]{2,1,0:T(4,128)S(1)}, u32[]{:S(2)}, u32[]{:S(2)}) async-start(f32[8,4,128]{2,1,0:T(4,128)} %bitcast.10), calls=%async_computation.3 | async-start | bytes 32768 | tf_op jit(solution)/shard_map/all_to_all | solution.py:126
  467.7 130.7 %collective-permute-start.4 = (f32[1024,128]{1,0:T(8,128)S(1)}, f32[1024,128]{1,0:T(8,128)S(1)}, u32[]{:S(2)}, u32[]{:S(2)}) collective-permute-start(f32[1024,128]{1,0:T(8,128)S(1)} %get-tuple-element.1693), channel_id=1, source_target_pairs={{8,0},{16,8},{24,16},{32,24},{40,32},{48,40},{56,48},{64,56},{72,6... | collective-permute-start | bytes 1572872 | tf_op jit(solution)/shard_map/ppermute | solution.py:17
  567.8 67.3 %collective-permute-start.5 = (f32[1024,128]{1,0:T(8,128)S(1)}, f32[1024,128]{1,0:T(8,128)S(1)}, u32[]{:S(2)}, u32[]{:S(2)}) collective-permute-start(f32[1024,128]{1,0:T(8,128)S(1)} %get-tuple-element.1694), channel_id=1, source_target_pairs={{16,0},{24,8},{32,16},{40,24},{48,32},{56,40},{64,48},{72,56},{80,... | collective-permute-start | bytes 1572872 | tf_op jit(solution)/shard_map/ppermute | solution.py:17
  572.9 77.7 %collective-permute-start.6 = (f32[1024,128]{1,0:T(8,128)}, f32[1024,128]{1,0:T(8,128)S(1)}, u32[]{:S(2)}, u32[]{:S(2)}) collective-permute-start(f32[1024,128]{1,0:T(8,128)} %get-tuple-element.1691), channel_id=1, source_target_pairs={{8,0},{16,8},{24,16},{32,24},{40,32},{48,40},{56,48},{64,56},{72,6... | collective-permute-start | bytes 1572872 | tf_op jit(solution)/shard_map/ppermute | solution.py:17
  574.8 93.4 %collective-permute-start.7 = (f32[1024,128]{1,0:T(8,128)}, f32[1024,128]{1,0:T(8,128)S(1)}, u32[]{:S(2)}, u32[]{:S(2)}) collective-permute-start(f32[1024,128]{1,0:T(8,128)} %get-tuple-element.1692), channel_id=1, source_target_pairs={{16,0},{24,8},{32,16},{40,24},{48,32},{56,40},{64,48},{72,56},{80,... | collective-permute-start | bytes 1572872 | tf_op jit(solution)/shard_map/ppermute | solution.py:17
  636.9 32.1 %all-to-all-start.6 = ((bf16[8,128,128]{2,1,0:T(8,128)(2,1)}), bf16[8,128,128]{2,1,0:T(8,128)(2,1)S(1)}, u32[]{:S(2)}, u32[]{:S(2)}) async-start(bf16[8,128,128]{2,1,0:T(8,128)(2,1)} %bitcast.20), calls=%async_computation.6 | async-start | bytes 524288 | tf_op jit(solution)/shard_map/all_to_all | solution.py:203
  669.0 11.5 %all-to-all-start.7 = ((bf16[8,128,128]{2,1,0:T(8,128)(2,1)}), bf16[8,128,128]{2,1,0:T(8,128)(2,1)S(1)}, u32[]{:S(2)}, u32[]{:S(2)}) async-start(bf16[8,128,128]{2,1,0:T(8,128)(2,1)} %bitcast.23), calls=%async_computation.7 | async-start | bytes 524288 | tf_op jit(solution)/shard_map/all_to_all | solution.py:204
  680.6 15.0 %all-to-all-start.5 = ((bf16[8,128,512]{2,1,0:T(8,128)(2,1)}), bf16[8,128,512]{2,1,0:T(8,128)(2,1)S(1)}, u32[]{:S(2)}, u32[]{:S(2)}) async-start(bf16[8,128,512]{2,1,0:T(8,128)(2,1)} %convert_element_type.58), calls=%async_computation.5 | async-start | bytes 2097152 | tf_op jit(solution)/shard_map/all_to_all | solution.py:202

commit v2 on v1

v2 whole, which is shorter than its diff:
```python
import jax
import jax.numpy as jnp
from jax import lax
from jax.experimental import pallas as pl
from jax.experimental.pallas import tpu as pltpu
from jax.sharding import PartitionSpec as P

HEAD_DIM = 128
TILE = 256
NEG_FILL = -1e30
ATT_SCALE = HEAD_DIM ** (-0.5)
LOG2E = 1.4426950408889634


def passed_along(block, axis, distance):
    devices = range(lax.axis_size(axis))
    route = [(i - distance, i) for i in devices if i - distance in devices]
    return lax.ppermute(block, axis, route)


def contract_last(left, right):
    return lax.dot_general(
        left, right, (((1,), (1,)), ((), ())), preferred_element_type=jnp.float32
    )


def contract_inner(left, right):
    return jnp.dot(left, right, preferred_element_type=jnp.float32)


def attention_kernel(
    first_tile,
    q_ref,
    g_ref,
    k_ref,
    v_ref,
    delta_ref,
    start_ref,
    dq_ref,
    dk_ref,
    dv_ref,
    kt_ref,
    score_ref,
):
    rows = q_ref.shape[0]
    heads = q_ref.shape[1] // HEAD_DIM
    halo_tiles = (k_ref.shape[0] - rows) // TILE
    dk_ref[...] = jnp.zeros_like(dk_ref)
    dv_ref[...] = jnp.zeros_like(dv_ref)
    key_offset = lax.broadcasted_iota(jnp.int32, (TILE, TILE), 0)
    query_offset = lax.broadcasted_iota(jnp.int32, (1, TILE), 1)

    def turn(tile, carry):
        at = pl.ds(pl.multiple_of(tile * TILE, TILE), TILE)
        kt_ref[:, at] = k_ref[at, :].T
        return carry

    lax.fori_loop(first_tile[0], k_ref.shape[0] // TILE, turn, 0)

    def query_block(block, carry):
        q_at = pl.ds(pl.multiple_of(block * TILE, TILE), TILE)
        low = first_tile[block]
        high = halo_tiles + block + 1
        start = start_ref[:, q_at]
        last = query_offset + (halo_tiles + block) * TILE
        for head in range(heads):
            cols = slice(head * HEAD_DIM, (head + 1) * HEAD_DIM)
            q = q_ref[q_at, cols]
            g = g_ref[q_at, cols]
            delta = delta_ref[head : head + 1, q_at]

            def score_step(tile, top):
                at = pl.ds(pl.multiple_of(tile * TILE, TILE), TILE)
                scores = contract_last(k_ref[at, :], q) * (ATT_SCALE * LOG2E)
                place = key_offset + tile * TILE
                scores = jnp.where((place >= start) & (place <= last), scores, NEG_FILL)
                score_ref[at, :] = scores
                return jnp.maximum(top, jnp.max(scores.reshape(TILE // 8, 8, TILE), axis=0))

            top = lax.fori_loop(low, high, score_step, jnp.full((8, TILE), NEG_FILL, jnp.float32))
            top = jnp.max(top, axis=0, keepdims=True)

            def sum_step(tile, total):
                at = pl.ds(pl.multiple_of(tile * TILE, TILE), TILE)
                powers = jnp.exp2(score_ref[at, :] - top)
                return total + jnp.sum(powers.reshape(TILE // 8, 8, TILE), axis=0)

            total = lax.fori_loop(low, high, sum_step, jnp.zeros((8, TILE), jnp.float32))
            log_total = top + jnp.log2(jnp.sum(total, axis=0, keepdims=True))

            def grad_step(tile, dq_turned):
                at = pl.ds(pl.multiple_of(tile * TILE, TILE), TILE)
                probs = jnp.exp2(score_ref[at, :] - log_total)
                grad_probs = contract_last(v_ref[at, :], g)
                grad_scores = (probs * (grad_probs - delta)).astype(jnp.bfloat16)
                dv_ref[at, :] += contract_inner(probs.astype(jnp.bfloat16), g)
                dk_ref[at, :] += contract_inner(grad_scores, q)
                return dq_turned + contract_inner(kt_ref[:, at], grad_scores)

            dq_turned = lax.fori_loop(
                low, high, grad_step, jnp.zeros((HEAD_DIM, TILE), jnp.float32)
            )
            dq_ref[q_at, cols] = (dq_turned.T * ATT_SCALE).astype(jnp.bfloat16)
        return carry

    lax.fori_loop(0, rows // TILE, query_block, 0)


def attention(first_tile, q, g, keys, vals, delta, starts):
    rows, window = q.shape[0], keys.shape[0]
    vmem = pl.BlockSpec(memory_space=pltpu.VMEM)
    return pl.pallas_call(
        attention_kernel,
        out_shape=(
            jax.ShapeDtypeStruct(q.shape, jnp.bfloat16),
            jax.ShapeDtypeStruct(keys.shape, jnp.float32),
            jax.ShapeDtypeStruct(keys.shape, jnp.float32),
        ),
        in_specs=[pl.BlockSpec(memory_space=pltpu.SMEM)] + [vmem] * 6,
        out_specs=(vmem, vmem, vmem),
        scratch_shapes=[
            pltpu.VMEM((HEAD_DIM, window), jnp.bfloat16),
            pltpu.VMEM((window, TILE), jnp.float32),
        ],
        compiler_params=pltpu.CompilerParams(vmem_limit_bytes=40 * 1024 * 1024),
        name="attention",
    )(first_tile, q, g, keys, vals, delta, starts)


def on_device(queries, keys, values, grad_out, delta, doc_lengths):
    q_local, k_local, v_local, g_local = (
        lax.all_to_all(queries, "head", split_axis=1, concat_axis=0, tiled=True),
        lax.all_to_all(keys, "head", split_axis=1, concat_axis=0, tiled=True),
        lax.all_to_all(values, "head", split_axis=1, concat_axis=0, tiled=True),
        lax.all_to_all(grad_out, "head", split_axis=1, concat_axis=0, tiled=True),
    )
    d_local = lax.all_to_all(delta, "head", split_axis=0, concat_axis=1, tiled=True)
    rows = q_local.shape[0]
    near_keys, near_vals = passed_along((k_local, v_local), "ctx", 1)
    far_keys, far_vals = passed_along((k_local, v_local), "ctx", 2)
    win_keys = jnp.concatenate([far_keys, near_keys, k_local], axis=0)
    win_vals = jnp.concatenate([far_vals, near_vals, v_local], axis=0)
    base = lax.axis_index("ctx") * rows
    slots = jnp.arange(doc_lengths.shape[0], dtype=jnp.int32)
    doc_starts = jnp.sum(jnp.where(slots[:, None] < slots[None, :], doc_lengths[:, None], 0), axis=0)
    places = base + jnp.arange(rows, dtype=jnp.int32)
    starts = jnp.max(jnp.where(doc_starts[:, None] <= places[None, :], doc_starts[:, None], 0), axis=0)
    starts = starts - (base - 2 * rows)
    first_tile = starts[::TILE] // TILE
    dq, dk, dv = attention(first_tile, q_local, g_local, win_keys, win_vals, d_local, starts[None])
    got_keys, got_vals = passed_along((dk[rows : 2 * rows], dv[rows : 2 * rows]), "ctx", -1)
    far_got_keys, far_got_vals = passed_along((dk[:rows], dv[:rows]), "ctx", -2)
    dk_low = ((dk[2 * rows :] + got_keys + far_got_keys) * ATT_SCALE).astype(jnp.bfloat16)
    dv_low = (dv[2 * rows :] + got_vals + far_got_vals).astype(jnp.bfloat16)
    return (
        lax.all_to_all(dq, "head", split_axis=0, concat_axis=1, tiled=True),
        lax.all_to_all(dk_low, "head", split_axis=0, concat_axis=1, tiled=True),
        lax.all_to_all(dv_low, "head", split_axis=0, concat_axis=1, tiled=True),
    )


def solution(mesh):
    rows = P(("ctx", "head"), None)
    return jax.shard_map(
        on_device,
        mesh=mesh,
        in_specs=(rows, rows, rows, rows, P(None, ("ctx", "head")), P()),
        out_specs=(rows, rows, rows),
        check_vma=False,
    )
```

time: 707 us -> 269 us (0.38)
  the two profiles are of different devices: /device:TPU:272 before, /device:TPU:8 now
where the time goes in v2:
time: 269 us; the launch traced here: 268 us
  waiting for transfers between devices  122 us (45%)
  starting transfers between devices  89.2 us (33%)
  Pallas kernels  29.5 us (11%)
  blocking collectives  13.4 us (5%)
  local copies, waits for them, and re-layouts  8.6 us (3%)
  other arithmetic  4.35 us (2%)
    ppermute x8, waiting for transfers between devices, passed_along(): return lax.ppermute(block, axis, route)  76.1 us
    all_to_all x1, starting transfers between devices, on_device(): lax.all_to_all(dk_low, 'head', split_axis=0, concat_axis=1, tiled=True)  39.4 us
    pallas_call x1, Pallas kernels, attention(): pl.pallas_call(attention_kernel, out_shape=(jax.ShapeDtypeStruct(q.shape,...  29.5 us
    ppermute x8, starting transfers between devices, passed_along(): return lax.ppermute(block, axis, route)  16.1 us
    all_to_all x1, blocking collectives, on_device(): lax.all_to_all(dv_low, 'head', split_axis=0, concat_axis=1, tiled=True)  13.4 us
    all_to_all x1, waiting for transfers between devices, on_device(): lax.all_to_all(grad_out, 'head', split_axis=1, concat_axis=0, tiled=True)  9.7 us
    all_to_all x1, waiting for transfers between devices, on_device(): lax.all_to_all(queries, 'head', split_axis=1, concat_axis=0, tiled=True)  9.25 us
    all_to_all x1, starting transfers between devices, on_device(): lax.all_to_all(delta, 'head', split_axis=0, concat_axis=1, tiled=True)  9.2 us
  transfers between devices with their start and end apart: 15, of which 11 were waited for; matrix products, arithmetic and copies ran while one was open for 4% of the time, Pallas kernels for 0%

profile of v2, /device:TPU:8, one launch (start us, length us, event | category | flops | bytes accessed | tf_op | source)
XLA Modules:
  0.0 267.6 jit_solution(7797347673197340443)
XLA Ops:
  0.6 0.0 copy-start
  0.6 0.0 copy-start.3
  0.7 9.2 %all-to-all-start.4 = ((f32[8,4,128]{2,1,0:T(4,128)}), f32[8,4,128]{2,1,0:T(4,128)S(1)}, u32[]{:S(2)}, u32[]{:S(2)}) async-start(f32[8,4,128]{2,1,0:T(4,128)} %bitcast.68), calls=%async_computation.4 | async-start | bytes 32768 | tf_op jit(solution)/shard_map/all_to_all | solution.py:137
  9.9 0.0 copy-done
  9.9 0.8 copy_bitcast_fusion.5
  10.6 4.1 %all-to-all-done.4 = f32[8,4,128]{2,1,0:T(4,128)S(1)} async-done(((f32[8,4,128]{2,1,0:T(4,128)}), f32[8,4,128]{2,1,0:T(4,128)S(1)}, u32[]{:S(2)}, u32[]{:S(2)}) %all-to-all-start.4) | async-done | bytes 16416 | tf_op jit(solution)/shard_map/all_to_all | solution.py:137
  14.7 4.7 %all-to-all-start.2 = ((bf16[128,8,128]{2,0,1:T(8,128)(2,1)}), bf16[128,8,128]{2,0,1:T(8,128)(2,1)S(1)}, u32[]{:S(2)}, u32[]{:S(2)}) async-start(bf16[128,8,128]{2,0,1:T(8,128)(2,1)} %copy_bitcast_fusion.5), calls=%async_computation.2 | async-start | bytes 524288 | tf_op jit(solution)/shard_map/all_to_all | solution.py:133
  19.4 1.7 copy_bitcast_fusion.4
  21.1 4.4 %all-to-all-done.2 = bf16[128,8,128]{2,0,1:T(8,128)(2,1)S(1)} async-done(((bf16[128,8,128]{2,0,1:T(8,128)(2,1)}), bf16[128,8,128]{2,0,1:T(8,128)(2,1)S(1)}, u32[]{:S(2)}, u32[]{:S(2)}) %all-to-all-start.2) | async-done | bytes 262176 | tf_op jit(solution)/shard_map/all_to_all | solution.py:133
  25.6 4.5 %all-to-all-start.3 = ((bf16[128,8,128]{2,0,1:T(8,128)(2,1)}), bf16[128,8,128]{2,0,1:T(8,128)(2,1)S(1)}, u32[]{:S(2)}, u32[]{:S(2)}) async-start(bf16[128,8,128]{2,0,1:T(8,128)(2,1)} %copy_bitcast_fusion.4), calls=%async_computation.3 | async-start | bytes 524288 | tf_op jit(solution)/shard_map/all_to_all | solution.py:134
  30.1 0.0 copy-done.3
  30.1 1.1 copy.45
  31.1 0.0 copy-start.4
  31.1 5.1 %all-to-all-done.3 = bf16[128,8,128]{2,0,1:T(8,128)(2,1)S(1)} async-done(((bf16[128,8,128]{2,0,1:T(8,128)(2,1)}), bf16[128,8,128]{2,0,1:T(8,128)(2,1)S(1)}, u32[]{:S(2)}, u32[]{:S(2)}) %all-to-all-start.3) | async-done | bytes 262176 | tf_op jit(solution)/shard_map/all_to_all | solution.py:134
  36.2 0.0 copy-start.5
  36.2 4.6 %all-to-all-start = ((bf16[128,8,512]{2,0,1:T(8,128)(2,1)}), bf16[128,8,512]{2,0,1:T(8,128)(2,1)S(1)}, u32[]{:S(2)}, u32[]{:S(2)}) async-start(bf16[128,8,512]{2,0,1:T(8,128)(2,1)} %bitcast.52), calls=%async_computation | async-start | bytes 2097152 | tf_op jit(solution)/shard_map/all_to_all | solution.py:132
  40.8 0.0 copy-done.4
  40.9 1.1 copy.44
  42.0 0.0 copy-start.6
  42.0 9.3 %all-to-all-done = bf16[128,8,512]{2,0,1:T(8,128)(2,1)S(1)} async-done(((bf16[128,8,512]{2,0,1:T(8,128)(2,1)}), bf16[128,8,512]{2,0,1:T(8,128)(2,1)S(1)}, u32[]{:S(2)}, u32[]{:S(2)}) %all-to-all-start) | async-done | bytes 1048608 | tf_op jit(solution)/shard_map/all_to_all | solution.py:132
  51.2 5.0 %all-to-all-start.1 = ((bf16[128,8,512]{2,0,1:T(8,128)(2,1)}), bf16[128,8,512]{2,0,1:T(8,128)(2,1)S(1)}, u32[]{:S(2)}, u32[]{:S(2)}) async-start(bf16[128,8,512]{2,0,1:T(8,128)(2,1)} %bitcast.51), calls=%async_computation.1 | async-start | bytes 2097152 | tf_op jit(solution)/shard_map/all_to_all | solution.py:135
  56.2 0.0 copy-done.6
  56.2 0.1 select_reduce_fusion.1
  56.4 0.2 select_reduce_fusion
  56.6 2.0 collective-permute-start.3
  58.6 0.0 copy-done.5
  58.6 2.3 collective-permute-start.2
  60.9 0.1 slice.21
  61.0 4.6 %collective-permute-start.1 = (bf16[1024,128]{1,0:T(8,128)(2,1)S(1)}, bf16[1024,128]{1,0:T(8,128)(2,1)S(1)}, u32[]{:S(2)}, u32[]{:S(2)}) collective-permute-start(bf16[1024,128]{1,0:T(8,128)(2,1)S(1)} %bitcast.62), channel_id=1, source_target_pairs={{0,8},{8,16},{16,24},{24,32},{32,40},{40,48},{48,56},{56,64},{64,7... | collective-permute-start | bytes 786440 | tf_op jit(solution)/shard_map/ppermute | solution.py:18
  65.6 2.0 collective-permute-start
  67.6 0.0 collective-permute-done.3
  67.6 0.0 collective-permute-done.2
  67.7 1.2 pad_maximum_fusion.1.v_ref
  68.8 0.0 collective-permute-done.1
  68.8 5.5 %collective-permute-done = bf16[1024,128]{1,0:T(8,128)(2,1)S(1)} collective-permute-done((bf16[1024,128]{1,0:T(8,128)(2,1)S(1)}, bf16[1024,128]{1,0:T(8,128)(2,1)S(1)}, u32[]{:S(2)}, u32[]{:S(2)}) %collective-permute-start) | collective-permute-done | bytes 262176 | tf_op jit(solution)/shard_map/ppermute | solution.py:18
  74.4 0.9 pad_maximum_fusion.k_ref
  75.3 9.7 %all-to-all-done.1 = bf16[128,8,512]{2,0,1:T(8,128)(2,1)S(1)} async-done(((bf16[128,8,512]{2,0,1:T(8,128)(2,1)}), bf16[128,8,512]{2,0,1:T(8,128)(2,1)S(1)}, u32[]{:S(2)}, u32[]{:S(2)}) %all-to-all-start.1) | async-done | bytes 1048608 | tf_op jit(solution)/shard_map/all_to_all | solution.py:135
  85.0 0.0 copy-start.1
  85.0 1.1 copy-done.1
  86.1 29.5 %attention.1 = (bf16[1024,512]{1,0:T(8,128)(2,1)}, f32[3072,128]{1,0:T(8,128)S(1)}, f32[3072,128]{1,0:T(8,128)S(1)}) custom-call(s32[4]{0:T(128)S(1)} %and_select_fusion.first_tile, bf16[1024,512]{1,0:T(8,128)(2,1)S(1)} %bitcast.53, bf16[1024,512]{1,0:T(8,128)(2,1)S(1)} %bitcast.54, bf16[3072,128]{1,0:T(8,128)(2,1)S(1)} %copy-done.1, ...), custom_call_target="tpu_custom_call" | custom-call | tf_op jit(solution)/shard_map/attention/pallas_call | solution.py:112
  115.6 0.0 copy-start.2
  115.6 0.1 fusion.1
  115.7 1.3 collective-permute-start.4
  117.0 1.3 collective-permute-start.5
  118.3 0.1 fusion
  118.4 0.0 copy-done.2
  118.4 1.3 collective-permute-start.6
  119.7 1.3 collective-permute-start.7
  121.0 1.7 collective-permute-done.4
  122.7 66.5 %collective-permute-done.5 = f32[1024,128]{1,0:T(8,128)S(1)} collective-permute-done((f32[1024,128]{1,0:T(8,128)S(1)}, f32[1024,128]{1,0:T(8,128)S(1)}, u32[]{:S(2)}, u32[]{:S(2)}) %collective-permute-start.5) | collective-permute-done | bytes 524320 | tf_op jit(solution)/shard_map/ppermute | solution.py:18
  189.2 0.8 multiply_convert_fusion
  190.0 39.4 %all-to-all-start.6 = ((bf16[8,128,128]{2,1,0:T(8,128)(2,1)}), bf16[8,128,128]{2,1,0:T(8,128)(2,1)S(1)}, u32[]{:S(2)}, u32[]{:S(2)}) async-start(bf16[8,128,128]{2,1,0:T(8,128)(2,1)} %bitcast.16), calls=%async_computation.6 | async-start | bytes 524288 | tf_op jit(solution)/shard_map/all_to_all | solution.py:157
  229.4 0.0 collective-permute-done.6
  229.4 2.3 collective-permute-done.7
  231.7 1.1 add_convert_fusion
  232.9 4.4 %all-to-all-done.6 = bf16[8,128,128]{2,1,0:T(8,128)(2,1)S(1)} async-done(((bf16[8,128,128]{2,1,0:T(8,128)(2,1)}), bf16[8,128,128]{2,1,0:T(8,128)(2,1)S(1)}, u32[]{:S(2)}, u32[]{:S(2)}) %all-to-all-start.6) | async-done | bytes 262176 | tf_op jit(solution)/shard_map/all_to_all | solution.py:157
  237.3 13.4 %all_to_all.152 = bf16[8,128,128]{2,1,0:T(8,128)(2,1)S(1)} all-to-all(bf16[8,128,128]{2,1,0:T(8,128)(2,1)S(1)} %bitcast.58), channel_id=1, replica_groups=mesh['ctx'=64,'head'=8] {'head'}, dimensions={0} | all-to-all | bytes 524288 | tf_op jit(solution)/shard_map/all_to_all | solution.py:158
  250.7 5.5 %all-to-all-start.5 = ((bf16[8,128,512]{2,1,0:T(8,128)(2,1)}), bf16[8,128,512]{2,1,0:T(8,128)(2,1)S(1)}, u32[]{:S(2)}, u32[]{:S(2)}) async-start(bf16[8,128,512]{2,1,0:T(8,128)(2,1)} %bitcast.14), calls=%async_computation.5 | async-start | bytes 2097152 | tf_op jit(solution)/shard_map/all_to_all | solution.py:156
  256.2 0.7 copy_bitcast_fusion.3
  257.0 0.7 copy_bitcast_fusion.2
  257.7 8.8 %all-to-all-done.5 = bf16[8,128,512]{2,1,0:T(8,128)(2,1)S(1)} async-done(((bf16[8,128,512]{2,1,0:T(8,128)(2,1)}), bf16[8,128,512]{2,1,0:T(8,128)(2,1)S(1)}, u32[]{:S(2)}, u32[]{:S(2)}) %all-to-all-start.5) | async-done | bytes 1048608 | tf_op jit(solution)/shard_map/all_to_all | solution.py:156
  266.6 1.1 copy.35
  (3 shorter events, 0.0 us)
Async XLA Ops:
  0.6 9.2 %copy-start = (bf16[128,1024]{1,0:T(8,128)(2,1)S(1)}, bf16[128,1024]{1,0:T(8,128)(2,1)}, u32[]{:S(2)}) copy-start(bf16[128,1024]{1,0:T(8,128)(2,1)} %param.7) | copy-start | bytes 786436
  0.6 29.4 %copy-start.3 = (bf16[128,4096]{1,0:T(8,128)(2,1)S(1)}, bf16[128,4096]{1,0:T(8,128)(2,1)}, u32[]{:S(2)}) copy-start(bf16[128,4096]{1,0:T(8,128)(2,1)} %param.6) | copy-start | bytes 3145732
  0.7 14.0 %all-to-all-start.4 = ((f32[8,4,128]{2,1,0:T(4,128)}), f32[8,4,128]{2,1,0:T(4,128)S(1)}, u32[]{:S(2)}, u32[]{:S(2)}) async-start(f32[8,4,128]{2,1,0:T(4,128)} %bitcast.68), calls=%async_computation.4 | async-start | bytes 32768 | tf_op jit(solution)/shard_map/all_to_all | solution.py:137
  14.7 10.9 %all-to-all-start.2 = ((bf16[128,8,128]{2,0,1:T(8,128)(2,1)}), bf16[128,8,128]{2,0,1:T(8,128)(2,1)S(1)}, u32[]{:S(2)}, u32[]{:S(2)}) async-start(bf16[128,8,128]{2,0,1:T(8,128)(2,1)} %copy_bitcast_fusion.5), calls=%async_computation.2 | async-start | bytes 524288 | tf_op jit(solution)/shard_map/all_to_all | solution.py:133
  25.6 10.6 %all-to-all-start.3 = ((bf16[128,8,128]{2,0,1:T(8,128)(2,1)}), bf16[128,8,128]{2,0,1:T(8,128)(2,1)S(1)}, u32[]{:S(2)}, u32[]{:S(2)}) async-start(bf16[128,8,128]{2,0,1:T(8,128)(2,1)} %copy_bitcast_fusion.4), calls=%async_computation.3 | async-start | bytes 524288 | tf_op jit(solution)/shard_map/all_to_all | solution.py:134
  31.1 9.7 %copy-start.4 = (bf16[128,4096]{1,0:T(8,128)(2,1)S(1)}, bf16[128,4096]{1,0:T(8,128)(2,1)}, u32[]{:S(2)}) copy-start(bf16[128,4096]{1,0:T(8,128)(2,1)} %param.9) | copy-start | bytes 3145732
  36.2 22.4 %copy-start.5 = (bf16[128,8,128]{2,0,1:T(8,128)(2,1)}, bf16[128,8,128]{2,0,1:T(8,128)(2,1)S(1)}, u32[]{:S(2)}) copy-start(bf16[128,8,128]{2,0,1:T(8,128)(2,1)S(1)} %all-to-all-done.3) | copy-start | bytes 786436
  36.2 15.0 %all-to-all-start = ((bf16[128,8,512]{2,0,1:T(8,128)(2,1)}), bf16[128,8,512]{2,0,1:T(8,128)(2,1)S(1)}, u32[]{:S(2)}, u32[]{:S(2)}) async-start(bf16[128,8,512]{2,0,1:T(8,128)(2,1)} %bitcast.52), calls=%async_computation | async-start | bytes 2097152 | tf_op jit(solution)/shard_map/all_to_all | solution.py:132
  42.0 14.3 %copy-start.6 = (s32[256]{0:T(256)S(1)}, s32[256]{0:T(256)}, u32[]{:S(2)}) copy-start(s32[256]{0:T(256)} %param.11) | copy-start | bytes 3076
  51.2 33.8 %all-to-all-start.1 = ((bf16[128,8,512]{2,0,1:T(8,128)(2,1)}), bf16[128,8,512]{2,0,1:T(8,128)(2,1)S(1)}, u32[]{:S(2)}, u32[]{:S(2)}) async-start(bf16[128,8,512]{2,0,1:T(8,128)(2,1)} %bitcast.51), calls=%async_computation.1 | async-start | bytes 2097152 | tf_op jit(solution)/shard_map/all_to_all | solution.py:135
  56.6 11.0 %collective-permute-start.3 = (bf16[1024,128]{1,0:T(8,128)(2,1)S(1)}, bf16[1024,128]{1,0:T(8,128)(2,1)}, u32[]{:S(2)}, u32[]{:S(2)}) collective-permute-start(bf16[1024,128]{1,0:T(8,128)(2,1)S(1)} %bitcast.65), channel_id=1, source_target_pairs={{0,8},{8,16},{16,24},{24,32},{32,40},{40,48},{48,56},{56,64},{64,7... | collective-permute-start | bytes 786440 | tf_op jit(solution)/shard_map/ppermute | solution.py:18
  58.6 9.0 %collective-permute-start.2 = (bf16[1024,128]{1,0:T(8,128)(2,1)S(1)}, bf16[1024,128]{1,0:T(8,128)(2,1)}, u32[]{:S(2)}, u32[]{:S(2)}) collective-permute-start(bf16[1024,128]{1,0:T(8,128)(2,1)S(1)} %bitcast.66), channel_id=1, source_target_pairs={{0,16},{8,24},{16,32},{24,40},{32,48},{40,56},{48,64},{56,72},{64,... | collective-permute-start | bytes 786440 | tf_op jit(solution)/shard_map/ppermute | solution.py:18
  61.0 7.8 %collective-permute-start.1 = (bf16[1024,128]{1,0:T(8,128)(2,1)S(1)}, bf16[1024,128]{1,0:T(8,128)(2,1)S(1)}, u32[]{:S(2)}, u32[]{:S(2)}) collective-permute-start(bf16[1024,128]{1,0:T(8,128)(2,1)S(1)} %bitcast.62), channel_id=1, source_target_pairs={{0,8},{8,16},{16,24},{24,32},{32,40},{40,48},{48,56},{56,64},{64,7... | collective-permute-start | bytes 786440 | tf_op jit(solution)/shard_map/ppermute | solution.py:18
  65.6 8.7 %collective-permute-start = (bf16[1024,128]{1,0:T(8,128)(2,1)S(1)}, bf16[1024,128]{1,0:T(8,128)(2,1)S(1)}, u32[]{:S(2)}, u32[]{:S(2)}) collective-permute-start(bf16[1024,128]{1,0:T(8,128)(2,1)S(1)} %bitcast.63), channel_id=1, source_target_pairs={{0,16},{8,24},{16,32},{24,40},{32,48},{40,56},{48,64},{56,72},{64,... | collective-permute-start | bytes 786440 | tf_op jit(solution)/shard_map/ppermute | solution.py:18
  85.0 1.1 copy-start.1
  115.6 2.8 %copy-start.2 = (f32[3072,128]{1,0:T(8,128)}, f32[3072,128]{1,0:T(8,128)S(1)}, u32[]{:S(2)}) copy-start(f32[3072,128]{1,0:T(8,128)S(1)} %get-tuple-element.8) | copy-start | bytes 4718596
  115.7 7.0 %collective-permute-start.4 = (f32[1024,128]{1,0:T(8,128)S(1)}, f32[1024,128]{1,0:T(8,128)S(1)}, u32[]{:S(2)}, u32[]{:S(2)}) collective-permute-start(f32[1024,128]{1,0:T(8,128)S(1)} %get-tuple-element.11), channel_id=1, source_target_pairs={{8,0},{16,8},{24,16},{32,24},{40,32},{48,40},{56,48},{64,56},{72,6... | collective-permute-start | bytes 1572872 | tf_op jit(solution)/shard_map/ppermute | solution.py:18
  117.0 72.2 %collective-permute-start.5 = (f32[1024,128]{1,0:T(8,128)S(1)}, f32[1024,128]{1,0:T(8,128)S(1)}, u32[]{:S(2)}, u32[]{:S(2)}) collective-permute-start(f32[1024,128]{1,0:T(8,128)S(1)} %get-tuple-element.12), channel_id=1, source_target_pairs={{16,0},{24,8},{32,16},{40,24},{48,32},{56,40},{64,48},{72,56},{80,... | collective-permute-start | bytes 1572872 | tf_op jit(solution)/shard_map/ppermute | solution.py:18
  118.4 111.0 %collective-permute-start.6 = (f32[1024,128]{1,0:T(8,128)S(1)}, f32[1024,128]{1,0:T(8,128)S(1)}, u32[]{:S(2)}, u32[]{:S(2)}) collective-permute-start(f32[1024,128]{1,0:T(8,128)S(1)} %get-tuple-element.9), channel_id=1, source_target_pairs={{8,0},{16,8},{24,16},{32,24},{40,32},{48,40},{56,48},{64,56},{72,6... | collective-permute-start | bytes 1572872 | tf_op jit(solution)/shard_map/ppermute | solution.py:18
  119.7 112.1 %collective-permute-start.7 = (f32[1024,128]{1,0:T(8,128)S(1)}, f32[1024,128]{1,0:T(8,128)S(1)}, u32[]{:S(2)}, u32[]{:S(2)}) collective-permute-start(f32[1024,128]{1,0:T(8,128)S(1)} %get-tuple-element.10), channel_id=1, source_target_pairs={{16,0},{24,8},{32,16},{40,24},{48,32},{56,40},{64,48},{72,56},{80,... | collective-permute-start | bytes 1572872 | tf_op jit(solution)/shard_map/ppermute | solution.py:18
  190.0 47.3 %all-to-all-start.6 = ((bf16[8,128,128]{2,1,0:T(8,128)(2,1)}), bf16[8,128,128]{2,1,0:T(8,128)(2,1)S(1)}, u32[]{:S(2)}, u32[]{:S(2)}) async-start(bf16[8,128,128]{2,1,0:T(8,128)(2,1)} %bitcast.16), calls=%async_computation.6 | async-start | bytes 524288 | tf_op jit(solution)/shard_map/all_to_all | solution.py:157
  250.7 15.9 %all-to-all-start.5 = ((bf16[8,128,512]{2,1,0:T(8,128)(2,1)}), bf16[8,128,512]{2,1,0:T(8,128)(2,1)S(1)}, u32[]{:S(2)}, u32[]{:S(2)}) async-start(bf16[8,128,512]{2,1,0:T(8,128)(2,1)} %bitcast.14), calls=%async_computation.5 | async-start | bytes 2097152 | tf_op jit(solution)/shard_map/all_to_all | solution.py:156

commit v3 on v2

v3 whole, which is shorter than its diff:
```python
import functools

import jax
import jax.numpy as jnp
from jax import lax
from jax.experimental import pallas as pl
from jax.experimental.pallas import tpu as pltpu
from jax.sharding import PartitionSpec as P

HEAD_DIM = 128
TILE = 256
STEP = 512
REACH = 2
NEG_FILL = -1e30
ATT_SCALE = HEAD_DIM ** (-0.5)
LOG2E = 1.4426950408889634
MESH = pl.DeviceIdType.MESH
VMEM = pl.BlockSpec(memory_space=pltpu.VMEM)
ANYWHERE = pl.BlockSpec(memory_space=pl.ANY)


def long_firsts(shards):
    middle = shards // 2
    return (0, middle - 3, middle - 1, middle + 1, shards - 3)


def halo_plan(shards, rows, short):
    near = tuple(range(shards - 1))
    far = tuple(range(shards - 2))
    if not short:
        return ((1, 0, rows, near), (2, 0, rows, far))
    firsts = long_firsts(shards)
    seconds = tuple(first + 1 for first in firsts)
    half = rows // 2
    return (
        (1, rows - TILE, rows, near),
        (1, half, rows - TILE, tuple(sorted(set(firsts + seconds)))),
        (1, 0, half, seconds),
        (2, half, rows, firsts),
    )


def halo_reach(shards, rows):
    half = rows // 2
    reach = [TILE] * shards
    for first in long_firsts(shards):
        reach[first + 1] = max(reach[first + 1], half)
        reach[first + 2] = max(reach[first + 2], rows + half)
    return reach


def is_one_of(index, members, shards):
    if members == tuple(range(len(members))):
        return index < len(members)
    return functools.reduce(jnp.logical_or, [index == member for member in members])


def contract_last(left, right):
    return lax.dot_general(
        left, right, (((1,), (1,)), ((), ())), preferred_element_type=jnp.float32
    )


def contract_inner(left, right):
    return jnp.dot(left, right, preferred_element_type=jnp.float32)


def meet(shards, peers, upward):
    ctx, head = lax.axis_index("ctx"), lax.axis_index("head")
    barrier = pltpu.get_barrier_semaphore()
    for step in range(1, peers):
        pl.semaphore_signal(
            barrier, inc=1, device_id=(ctx, lax.rem(head + step, peers)), device_id_type=MESH
        )
    for distance in (1, 2):
        other = ctx - distance if upward else ctx + distance
        there = ctx >= distance if upward else ctx < shards - distance

        @pl.when(there)
        def _():
            pl.semaphore_signal(barrier, inc=1, device_id=(other, head), device_id_type=MESH)

    beyond = shards - 1 - ctx if upward else ctx
    pl.semaphore_wait(barrier, peers - 1 + jnp.minimum(beyond, REACH))


def gather_kernel(
    shards,
    plan,
    q_in,
    k_in,
    v_in,
    g_in,
    d_in,
    q_out,
    k_out,
    v_out,
    g_out,
    d_out,
    send_sem,
    recv_sem,
    local_sem,
    halo_send,
    halo_recv,
):
    ctx, head = lax.axis_index("ctx"), lax.axis_index("head")
    part = q_in.shape[0]
    rows = q_out.shape[0]
    peers = rows // part
    halo = k_out.shape[0] - rows
    k_out[:halo, :] = jnp.zeros((halo, HEAD_DIM), k_out.dtype)
    v_out[:halo, :] = jnp.zeros((halo, HEAD_DIM), v_out.dtype)
    meet(shards, peers, True)

    def columns(ref, owner):
        width = ref.shape[1] // peers
        return ref.at[:, pl.ds(pl.multiple_of(owner * width, width), width)]

    def own_rows(ref, owner, first):
        return ref.at[pl.ds(pl.multiple_of(first + owner * part, part), part), :]

    pairs = (
        (lambda to: columns(k_in, to), lambda of: own_rows(k_out, of, halo)),
        (lambda to: columns(v_in, to), lambda of: own_rows(v_out, of, halo)),
        (lambda to: d_in.at[to], lambda of: d_out.at[of]),
        (lambda to: columns(q_in, to), lambda of: own_rows(q_out, of, 0)),
        (lambda to: columns(g_in, to), lambda of: own_rows(g_out, of, 0)),
    )

    def exchange(index, step):
        to = lax.rem(head + step, peers)
        source, target = pairs[index]
        return pltpu.make_async_remote_copy(
            src_ref=source(to),
            dst_ref=target(head),
            send_sem=send_sem.at[index, step],
            recv_sem=recv_sem.at[index, step],
            device_id=(ctx, to),
            device_id_type=MESH,
        )

    def keep(index):
        source, target = pairs[index]
        return pltpu.make_async_copy(source(head), target(head), local_sem.at[index])

    def arrived(index, step):
        source, target = pairs[index]
        of = lax.rem(head + peers - step, peers)
        pltpu.make_async_remote_copy(
            src_ref=source(head),
            dst_ref=target(of),
            send_sem=send_sem.at[index, step],
            recv_sem=recv_sem.at[index, step],
            device_id=(ctx, of),
            device_id_type=MESH,
        ).wait_recv()

    for index in range(5):
        keep(index).start()
        for step in range(1, peers):
            exchange(index, step).start()
    for index in range(2):
        keep(index).wait()
        for step in range(1, peers):
            arrived(index, step)

    def halo_copy(run, which):
        distance, first, end, _ = plan[run]
        ref = (k_out, v_out)[which]
        return pltpu.make_async_remote_copy(
            src_ref=ref.at[halo + first : halo + end, :],
            dst_ref=ref.at[halo - distance * rows + first : halo - distance * rows + end, :],
            send_sem=halo_send.at[run, which],
            recv_sem=halo_recv.at[run, which],
            device_id=(ctx + distance, head),
            device_id_type=MESH,
        )

    for run, (distance, first, end, senders) in enumerate(plan):

        @pl.when(is_one_of(ctx, senders, shards))
        def _():
            for which in range(2):
                halo_copy(run, which).start()

    for index in range(2, 5):
        keep(index).wait()
        for step in range(1, peers):
            arrived(index, step)
    for run, (distance, first, end, senders) in enumerate(plan):

        @pl.when(is_one_of(ctx, senders, shards))
        def _():
            for which in range(2):
                halo_copy(run, which).wait_send()

        @pl.when(is_one_of(ctx - distance, senders, shards) & (ctx >= distance))
        def _():
            for which in range(2):
                halo_copy(run, which).wait_recv()

    for index in range(5):
        for step in range(1, peers):
            exchange(index, step).wait_send()


def gather(shards, plan, short, queries, keys, values, grad_out, delta):
    peers = delta.shape[0]
    rows = queries.shape[0] * peers
    window = (REACH + 1) * rows + TILE
    width = queries.shape[1] // peers
    low = jnp.bfloat16
    return pl.pallas_call(
        functools.partial(gather_kernel, shards, plan),
        out_shape=(
            jax.ShapeDtypeStruct((rows, width), low),
            jax.ShapeDtypeStruct((window, HEAD_DIM), low),
            jax.ShapeDtypeStruct((window, HEAD_DIM), low),
            jax.ShapeDtypeStruct((rows, width), low),
            jax.ShapeDtypeStruct(delta.shape, jnp.float32),
        ),
        in_specs=[ANYWHERE] * 4 + [VMEM],
        out_specs=(VMEM,) * 5,
        scratch_shapes=[
            pltpu.SemaphoreType.DMA((5, peers)),
            pltpu.SemaphoreType.DMA((5, peers)),
            pltpu.SemaphoreType.DMA((5,)),
            pltpu.SemaphoreType.DMA((len(plan), 2)),
            pltpu.SemaphoreType.DMA((len(plan), 2)),
        ],
        compiler_params=pltpu.CompilerParams(
            collective_id=0 if short else 1,
            has_side_effects=True,
            vmem_limit_bytes=32 * 1024 * 1024,
        ),
        name="gather_short" if short else "gather_full",
    )(queries, keys, values, grad_out, delta)


def attention_kernel(
    first_row,
    q_ref,
    g_ref,
    k_ref,
    v_ref,
    delta_ref,
    start_ref,
    dq_ref,
    dk_ref,
    dv_ref,
    kt_ref,
    score_ref,
    turned_ref,
):
    rows = q_ref.shape[0]
    heads = range(q_ref.shape[1] // HEAD_DIM)
    halo = k_ref.shape[0] - rows
    parts = TILE // delta_ref.shape[2]
    columns = [slice(head * HEAD_DIM, (head + 1) * HEAD_DIM) for head in heads]
    dk_ref[...] = jnp.zeros_like(dk_ref)
    dv_ref[...] = jnp.zeros_like(dv_ref)
    key_offset = lax.broadcasted_iota(jnp.int32, (STEP, TILE), 0)
    query_offset = lax.broadcasted_iota(jnp.int32, (1, TILE), 1)

    def turn(tile, carry):
        at = pl.ds(pl.multiple_of(tile * TILE, TILE), TILE)
        kt_ref[:, at] = k_ref[at, :].T
        return carry

    lax.fori_loop(jnp.maximum(first_row[0] // TILE - 1, 0), k_ref.shape[0] // TILE, turn, 0)

    def query_block(block, carry):
        q_at = pl.ds(pl.multiple_of(block * TILE, TILE), TILE)
        end = halo + (block + 1) * TILE
        count = (end - first_row[block] + STEP - 1) // STEP
        start = start_ref[:, q_at]
        last = query_offset + (end - TILE)
        deltas = [
            jnp.concatenate(
                [delta_ref[block * parts + part, head : head + 1, :] for part in range(parts)],
                axis=1,
            )
            for head in heads
        ]

        def key_rows(step):
            return pl.multiple_of(end - (step + 1) * STEP, TILE)

        def score_step(step, tops):
            first = key_rows(step)
            at = pl.ds(first, STEP)
            keys = k_ref[at, :]
            place = key_offset + first
            allowed = (place >= start) & (place <= last)
            new_tops = []
            for head in heads:
                scores = contract_last(keys, q_ref[q_at, columns[head]]) * (ATT_SCALE * LOG2E)
                scores = jnp.where(allowed, scores, NEG_FILL)
                score_ref[head, at, :] = scores
                tall = jnp.max(scores.reshape(STEP // 8, 8, TILE), axis=0)
                new_tops.append(jnp.maximum(tops[head], tall))
            return tuple(new_tops)

        none = jnp.full((8, TILE), NEG_FILL, jnp.float32)
        tops = lax.fori_loop(0, count, score_step, tuple(none for _ in heads))
        tops = [jnp.max(top, axis=0, keepdims=True) for top in tops]

        def sum_step(step, totals):
            at = pl.ds(key_rows(step), STEP)
            new_totals = []
            for head in heads:
                powers = jnp.exp2(score_ref[head, at, :] - tops[head])
                new_totals.append(
                    totals[head] + jnp.sum(powers.reshape(STEP // 8, 8, TILE), axis=0)
                )
            return tuple(new_totals)

        zero = jnp.zeros((8, TILE), jnp.float32)
        totals = lax.fori_loop(0, count, sum_step, tuple(zero for _ in heads))
        log_totals = [
            tops[head] + jnp.log2(jnp.sum(totals[head], axis=0, keepdims=True)) for head in heads
        ]
        turned_ref[...] = jnp.zeros_like(turned_ref)

        def grad_step(step, carry):
            at = pl.ds(key_rows(step), STEP)
            vals = v_ref[at, :]
            keys_turned = kt_ref[:, at]
            val_parts, key_parts = [], []
            for head in heads:
                q = q_ref[q_at, columns[head]]
                g = g_ref[q_at, columns[head]]
                probs = jnp.exp2(score_ref[head, at, :] - log_totals[head])
                grad_probs = contract_last(vals, g)
                grad_scores = (probs * (grad_probs - deltas[head])).astype(jnp.bfloat16)
                val_parts.append(contract_inner(probs.astype(jnp.bfloat16), g))
                key_parts.append(contract_inner(grad_scores, q))
                turned_ref[head] += contract_inner(keys_turned, grad_scores)
            dv_ref[at, :] += sum(val_parts[1:], val_parts[0])
            dk_ref[at, :] += sum(key_parts[1:], key_parts[0])
            return carry

        lax.fori_loop(0, count, grad_step, 0)
        for head in heads:
            dq_ref[q_at, columns[head]] = (turned_ref[head].T * ATT_SCALE).astype(jnp.bfloat16)
        return carry

    lax.fori_loop(0, rows // TILE, query_block, 0)


def attention(first_row, q, g, keys, vals, delta, starts):
    window = keys.shape[0]
    heads = q.shape[1] // HEAD_DIM
    return pl.pallas_call(
        attention_kernel,
        out_shape=(
            jax.ShapeDtypeStruct(q.shape, jnp.bfloat16),
            jax.ShapeDtypeStruct(keys.shape, jnp.float32),
            jax.ShapeDtypeStruct(keys.shape, jnp.float32),
        ),
        in_specs=[pl.BlockSpec(memory_space=pltpu.SMEM)] + [VMEM] * 6,
        out_specs=(VMEM,) * 3,
        scratch_shapes=[
            pltpu.VMEM((HEAD_DIM, window), jnp.bfloat16),
            pltpu.VMEM((heads, window, TILE), jnp.float32),
            pltpu.VMEM((heads, HEAD_DIM, TILE), jnp.float32),
        ],
        compiler_params=pltpu.CompilerParams(vmem_limit_bytes=44 * 1024 * 1024),
        name="attention",
    )(first_row, q, g, keys, vals, delta, starts)


def scatter_kernel(
    shards,
    plan,
    dq_in,
    dk_in,
    dv_in,
    dq_out,
    dk_out,
    dv_out,
    low_ref,
    got_ref,
    total_ref,
    sum_ref,
    send_sem,
    recv_sem,
    local_sem,
    halo_send,
    halo_recv,
):
    ctx, head = lax.axis_index("ctx"), lax.axis_index("head")
    part = dq_out.shape[0]
    rows = dq_in.shape[0]
    peers = rows // part
    halo = dk_in.shape[0] - rows
    meet(shards, peers, False)

    def columns(ref, owner):
        width = ref.shape[1] // peers
        return ref.at[:, pl.ds(pl.multiple_of(owner * width, width), width)]

    def row_part(ref, owner):
        return ref.at[pl.ds(pl.multiple_of(owner * part, part), part), :]

    pairs = (
        (lambda to: row_part(dq_in, to), lambda of: columns(dq_out, of)),
        (lambda to: row_part(sum_ref.at[0], to), lambda of: columns(dk_out, of)),
        (lambda to: row_part(sum_ref.at[1], to), lambda of: columns(dv_out, of)),
    )

    def exchange(index, step):
        to = lax.rem(head + step, peers)
        source, target = pairs[index]
        return pltpu.make_async_remote_copy(
            src_ref=source(to),
            dst_ref=target(head),
            send_sem=send_sem.at[index, step],
            recv_sem=recv_sem.at[index, step],
            device_id=(ctx, to),
            device_id_type=MESH,
        )

    def keep(index):
        source, target = pairs[index]
        return pltpu.make_async_copy(source(head), target(head), local_sem.at[index])

    def arrived(index, step):
        source, target = pairs[index]
        of = lax.rem(head + peers - step, peers)
        pltpu.make_async_remote_copy(
            src_ref=source(head),
            dst_ref=target(of),
            send_sem=send_sem.at[index, step],
            recv_sem=recv_sem.at[index, step],
            device_id=(ctx, of),
            device_id_type=MESH,
        ).wait_recv()

    def halo_copy(run, which):
        distance, first, end, _ = plan[run]
        base = halo - distance * rows
        return pltpu.make_async_remote_copy(
            src_ref=low_ref.at[which, base + first : base + end, :],
            dst_ref=got_ref.at[which, base + first : base + end, :],
            send_sem=halo_send.at[run, which],
            recv_sem=halo_recv.at[run, which],
            device_id=(ctx - distance, head),
            device_id_type=MESH,
        )

    for run, (distance, first, end, senders) in enumerate(plan):

        @pl.when(is_one_of(ctx - distance, senders, shards) & (ctx >= distance))
        def _():
            at = slice(halo - distance * rows + first, halo - distance * rows + end)
            low_ref[0, at, :] = (dk_in[at, :] * ATT_SCALE).astype(jnp.bfloat16)
            low_ref[1, at, :] = dv_in[at, :].astype(jnp.bfloat16)
            for which in range(2):
                halo_copy(run, which).start()

    keep(0).start()
    for step in range(1, peers):
        exchange(0, step).start()
    total_ref[0] = dk_in[halo:, :] * ATT_SCALE
    total_ref[1] = dv_in[halo:, :]

    for run, (distance, first, end, senders) in enumerate(plan):

        @pl.when(is_one_of(ctx, senders, shards))
        def _():
            got = slice(halo - distance * rows + first, halo - distance * rows + end)
            own = slice(first, end)
            for which in range(2):
                halo_copy(run, which).wait_recv()
                total_ref[which, own, :] += got_ref[which, got, :].astype(jnp.float32)

    sum_ref[...] = total_ref[...].astype(jnp.bfloat16)
    for index in (1, 2):
        keep(index).start()
        for step in range(1, peers):
            exchange(index, step).start()
    for run, (distance, first, end, senders) in enumerate(plan):

        @pl.when(is_one_of(ctx - distance, senders, shards) & (ctx >= distance))
        def _():
            for which in range(2):
                halo_copy(run, which).wait_send()

    for index in range(3):
        keep(index).wait()
        for step in range(1, peers):
            arrived(index, step)
            exchange(index, step).wait_send()


def scatter(shards, plan, short, peers, dq, dk, dv):
    rows, width = dq.shape
    window = dk.shape[0]
    low = jnp.bfloat16
    return pl.pallas_call(
        functools.partial(scatter_kernel, shards, plan),
        out_shape=(
            jax.ShapeDtypeStruct((rows // peers, width * peers), low),
            jax.ShapeDtypeStruct((rows // peers, HEAD_DIM * peers), low),
            jax.ShapeDtypeStruct((rows // peers, HEAD_DIM * peers), low),
        ),
        in_specs=[VMEM] * 3,
        out_specs=(ANYWHERE,) * 3,
        scratch_shapes=[
            pltpu.VMEM((2, window - rows, HEAD_DIM), low),
            pltpu.VMEM((2, window - rows, HEAD_DIM), low),
            pltpu.VMEM((2, rows, HEAD_DIM), jnp.float32),
            pltpu.VMEM((2, rows, HEAD_DIM), low),
            pltpu.SemaphoreType.DMA((3, peers)),
            pltpu.SemaphoreType.DMA((3, peers)),
            pltpu.SemaphoreType.DMA((3,)),
            pltpu.SemaphoreType.DMA((len(plan), 2)),
            pltpu.SemaphoreType.DMA((len(plan), 2)),
        ],
        compiler_params=pltpu.CompilerParams(
            collective_id=2 if short else 3,
            has_side_effects=True,
            vmem_limit_bytes=32 * 1024 * 1024,
        ),
        name="scatter_short" if short else "scatter_full",
    )(dq, dk, dv)


def on_device(queries, keys, values, grad_out, delta, doc_lengths):
    shards, peers = lax.axis_size("ctx"), lax.axis_size("head")
    rows = queries.shape[0] * peers
    delta = delta.reshape(peers, delta.shape[0] // peers, delta.shape[1])
    slots = jnp.arange(doc_lengths.shape[0], dtype=jnp.int32)
    doc_starts = jnp.sum(jnp.where(slots[:, None] < slots[None, :], doc_lengths[:, None], 0), axis=0)

    def start_at(places):
        return jnp.max(
            jnp.where(doc_starts[:, None] <= places[None, :], doc_starts[:, None], 0), axis=0
        )

    base = lax.axis_index("ctx") * rows
    starts = start_at(base + jnp.arange(rows, dtype=jnp.int32)) - (base - REACH * rows - TILE)
    first_row = starts[::TILE]
    edges = jnp.arange(shards, dtype=jnp.int32) * rows
    reach = jnp.array(halo_reach(shards, rows), jnp.int32)
    fits = jnp.all(start_at(edges) >= edges - reach)

    def run(short, *operands):
        plan = halo_plan(shards, rows, short)
        q, k, v, g, d = gather(shards, plan, short, *operands)
        dq, dk, dv = attention(first_row, q, g, k, v, d, starts[None])
        return scatter(shards, plan, short, peers, dq, dk, dv)

    return lax.cond(
        fits,
        functools.partial(run, True),
        functools.partial(run, False),
        queries,
        keys,
        values,
        grad_out,
        delta,
    )


def solution(mesh):
    rows = P(("ctx", "head"), None)
    return jax.shard_map(
        on_device,
        mesh=mesh,
        in_specs=(rows, rows, rows, rows, P(None, ("ctx", "head")), P()),
        out_specs=(rows, rows, rows),
        check_vma=False,
    )
```

time: 269 us -> 120 us (0.45)
  the two profiles are of different devices: /device:TPU:8 before, /device:TPU:16 now
where the time goes in v3:
time: 120 us
  Pallas kernels  114 us (95%)
  other arithmetic  2.51 us (2%)
  local copies, waits for them, and re-layouts  2.47 us (2%)
  between operations  1.33 us (1%)
    pallas_call x1, Pallas kernels, gather(): pl.pallas_call(functools.partial(gather_kernel, shards, plan), out_shape=...  45.7 us
    pallas_call x1, Pallas kernels, attention(): pl.pallas_call(attention_kernel, out_shape=(jax.ShapeDtypeStruct(q.shape,...  34.4 us
    pallas_call x1, Pallas kernels, scatter(): pl.pallas_call(functools.partial(scatter_kernel, shards, plan), out_shape...  33.6 us

profile of v3, /device:TPU:16, one launch (start us, length us, event | category | flops | bytes accessed | tf_op | source)
XLA Modules:
  0.0 120.0 jit_solution(8303755582468106125)
XLA Ops:
  0.6 0.8 select_reduce_fusion.1
  1.4 0.2 select_reduce_fusion.2
  1.6 1.3 %compare_reduce_fusion = pred[]{:T(512)} fusion(s32[64]{0:T(128)S(1)} %select_reduce_fusion.2, s32[64]{0:T(128)} %constant.29), kind=kLoop, calls=%fused_computation.6 | loop fusion | flops 255 | bytes 513 | tf_op jit(solution)/shard_map/reduce_and | solution.py:547
  3.6 0.2 select_reduce_fusion
  3.8 113.8 %conditional.1 = ((bf16[128,4096]{1,0:T(8,128)(2,1)S(1)}, bf16[128,1024]{1,0:T(8,128)(2,1)S(1)}, bf16[128,1024]{1,0:T(8,128)(2,1)S(1)})) conditional(s32[]{:T(128)} %convert_element_type.3, (bf16[128,4096]{1,0:T(8,128)(2,1)}, bf16[128,1024]{1,0:T(8,128)(2,1)}, bf16[128,1024]{1,0:T(8,128)(2,1)}, bf16[128,4096]{1,0:T(8,128)(2,1)}, f32[32,128]{1,0:T(8,128)}, ...), branch_computations={%region_4.5_spmd, %region_5.6_spmd} | conditional | bytes 40 | solution.py:555
  3.9 0.1 slice.5.first_row
  3.9 45.7 %gather_short.1 = (bf16[1024,512]{1,0:T(8,128)(2,1)S(1)}, bf16[3328,128]{1,0:T(8,128)(2,1)S(1)}, bf16[3328,128]{1,0:T(8,128)(2,1)S(1)}, bf16[1024,512]{1,0:T(8,128)(2,1)S(1)}, f32[8,4,128]{2,1,0:T(4,128)S(1)}) custom-call(bf16[128,4096]{1,0:T(8,128)(2,1)} %get-tuple-element.83.q_in, bf16[128,1024]{1,0:T(8,128)(2,1)} %get-tuple-element.85.k_in, ...), custom_call_target="tpu_custom_call" | custom-call | tf_op jit(solution)/shard_map/cond/branch_1_fun/gather_short/pallas_call | solution.py:213
  49.6 34.4 %attention.3 = (bf16[1024,512]{1,0:T(8,128)(2,1)S(1)}, f32[3328,128]{1,0:T(8,128)S(1)}, f32[3328,128]{1,0:T(8,128)S(1)}) custom-call(s32[4]{0:T(128)S(1)} %slice.5.first_row, bf16[1024,512]{1,0:T(8,128)(2,1)S(1)} %get-tuple-element.49.q_ref, bf16[1024,512]{1,0:T(8,128)(2,1)S(1)} %get-tuple-element.50.g_ref, bf16[3328,128]{1,0:T(8,128)(2,1)S(1)} %get-tuple-element.51.k_ref, ...), custom_call_target="tpu_custom_call" | custom-call | tf_op jit(solution)/shard_map/cond/branch_1_fun/attention/pallas_call | solution.py:354
  84.0 33.6 %scatter_short.1 = (bf16[128,4096]{1,0:T(8,128)(2,1)S(1)}, bf16[128,1024]{1,0:T(8,128)(2,1)S(1)}, bf16[128,1024]{1,0:T(8,128)(2,1)S(1)}) custom-call(bf16[1024,512]{1,0:T(8,128)(2,1)S(1)} %get-tuple-element.55.dq_in, f32[3328,128]{1,0:T(8,128)S(1)} %get-tuple-element.56.dk_in, f32[3328,128]{1,0:T(8,128)S(1)} %get-tuple-element.57.dv_in), custom_call_target="tpu_custom_call" | custom-call | tf_op jit(solution)/shard_map/cond/branch_1_fun/scatter_short/pallas_call | solution.py:501
  117.6 1.0 copy.35
  118.6 0.7 copy.36
  119.3 0.7 copy.37
  (3 shorter events, 0.0 us)

commit v4 on v3

--- a/solution.py
+++ b/solution.py
@@ -2,6 +2,7 @@
 
 import jax
 import jax.numpy as jnp
+import numpy as np
 from jax import lax
 from jax.experimental import pallas as pl
 from jax.experimental.pallas import tpu as pltpu
@@ -40,12 +41,13 @@
     )
 
 
-def halo_reach(shards, rows):
-    half = rows // 2
-    reach = [TILE] * shards
+def short_reach(blocks, shards, rows):
+    shard = blocks * TILE // rows
+    reach = (blocks - 1) * TILE
     for first in long_firsts(shards):
-        reach[first + 1] = max(reach[first + 1], half)
-        reach[first + 2] = max(reach[first + 2], rows + half)
+        opening = first * rows + rows // 2
+        for other in (first + 1, first + 2):
+            reach = np.where(shard == other, np.minimum(reach, opening), reach)
     return reach
 
 
@@ -204,7 +206,7 @@
             exchange(index, step).wait_send()
 
 
-def gather(shards, plan, short, queries, keys, values, grad_out, delta):
+def gather(shards, plan, queries, keys, values, grad_out, delta):
     peers = delta.shape[0]
     rows = queries.shape[0] * peers
     window = (REACH + 1) * rows + TILE
@@ -229,11 +231,11 @@
             pltpu.SemaphoreType.DMA((len(plan), 2)),
         ],
         compiler_params=pltpu.CompilerParams(
-            collective_id=0 if short else 1,
+            collective_id=1,
             has_side_effects=True,
             vmem_limit_bytes=32 * 1024 * 1024,
         ),
-        name="gather_short" if short else "gather_full",
+        name="gather",
     )(queries, keys, values, grad_out, delta)
 
 
@@ -494,7 +496,7 @@
             exchange(index, step).wait_send()
 
 
-def scatter(shards, plan, short, peers, dq, dk, dv):
+def scatter(shards, plan, peers, dq, dk, dv):
     rows, width = dq.shape
     window = dk.shape[0]
     low = jnp.bfloat16
@@ -519,12 +521,408 @@
             pltpu.SemaphoreType.DMA((len(plan), 2)),
         ],
         compiler_params=pltpu.CompilerParams(
-            collective_id=2 if short else 3,
+            collective_id=2,
             has_side_effects=True,
             vmem_limit_bytes=32 * 1024 * 1024,
         ),
-        name="scatter_short" if short else "scatter_full",
+        name="scatter",
     )(dq, dk, dv)
+
+
+def first_tiles(ctx, block, shards, rows, reach_tiles):
+    own = rows // TILE
+    half = own // 2
+    firsts = long_firsts(shards)
+    second = is_one_of(ctx, tuple(first + 1 for first in firsts), shards)
+    third = is_one_of(ctx, tuple(first + 2 for first in firsts), shards)
+    low = jnp.where(second, jnp.minimum(reach_tiles - half, reach_tiles + block - 1), reach_tiles + block - 1)
+    return jnp.where(third, reach_tiles - own - half, low)
+
+
+def whole_kernel(
+    shards,
+    plan,
+    q_in,
+    k_in,
+    v_in,
+    g_in,
+    d_in,
+    lengths_ref,
+    dq_out,
+    dk_out,
+    dv_out,
+    q_buf,
+    g_buf,
+    k_win,
+    v_win,
+    d_buf,
+    start_ref,
+    kt_ref,
+    score_ref,
+    probs_ref,
+    grads_ref,
+    q_stack,
+    g_stack,
+    turned_ref,
+    dk_acc,
+    dv_acc,
+    dq_buf,
+    low_ref,
+    got_ref,
+    total_ref,
+    sum_ref,
+    send_sem,
+    recv_sem,
+    local_sem,
+    halo_send,
+    halo_recv,
+    back_send,
+    back_recv,
+):
+    ctx, head = lax.axis_index("ctx"), lax.axis_index("head")
+    part = q_in.shape[0]
+    rows, width = q_buf.shape
+    peers = rows // part
+    halo = k_win.shape[0] - rows
+    half_width = width // 2
+    pair_heads = range(half_width // HEAD_DIM)
+    stacks = [slice(one * TILE, (one + 1) * TILE) for one in pair_heads]
+    k_win[:halo, :] = jnp.zeros((halo, HEAD_DIM), k_win.dtype)
+    v_win[:halo, :] = jnp.zeros((halo, HEAD_DIM), v_win.dtype)
+
+    barrier = pltpu.get_barrier_semaphore()
+    for step in range(1, peers):
+        pl.semaphore_signal(
+            barrier, inc=1, device_id=(ctx, lax.rem(head + step, peers)), device_id_type=MESH
+        )
+    for distance in (1, 2):
+
+        @pl.when(ctx >= distance)
+        def _():
+            pl.semaphore_signal(
+                barrier, inc=1, device_id=(ctx - distance, head), device_id_type=MESH
+            )
+
+        @pl.when(ctx < shards - distance)
+        def _():
+            pl.semaphore_signal(
+                barrier, inc=1, device_id=(ctx + distance, head), device_id_type=MESH
+            )
+
+    around = jnp.minimum(shards - 1 - ctx, REACH) + jnp.minimum(ctx, REACH)
+    pl.semaphore_wait(barrier, peers - 1 + around)
+
+    def columns(ref, owner, offset, size):
+        stride = ref.shape[1] // peers
+        return ref.at[:, pl.ds(pl.multiple_of(owner * stride + offset, size), size)]
+
+    def own_rows(ref, owner, first):
+        return ref.at[pl.ds(pl.multiple_of(first + owner * part, part), part), :]
+
+    def own_pair(ref, owner, pair):
+        at = pl.ds(pl.multiple_of(owner * part, part), part)
+        return ref.at[at, pair * half_width : (pair + 1) * half_width]
+
+    def paired_in(source, target, pair):
+        return (
+            lambda to: columns(source, to, pair * half_width, half_width),
+            lambda of: own_pair(target, of, pair),
+        )
+
+    def paired_out(source, target, pair):
+        return (
+            lambda to: own_pair(source, to, pair),
+            lambda of: columns(target, of, pair * half_width, half_width),
+        )
+
+    routes = (
+        (lambda to: columns(k_in, to, 0, HEAD_DIM), lambda of: own_rows(k_win, of, halo)),
+        (lambda to: columns(v_in, to, 0, HEAD_DIM), lambda of: own_rows(v_win, of, halo)),
+        (lambda to: d_in.at[to], lambda of: d_buf.at[of]),
+        paired_in(q_in, q_buf, 0),
+        paired_in(g_in, g_buf, 0),
+        paired_in(q_in, q_buf, 1),
+        paired_in(g_in, g_buf, 1),
+        paired_out(dq_buf, dq_out, 0),
+        paired_out(dq_buf, dq_out, 1),
+        (lambda to: own_rows(sum_ref.at[0], to, 0), lambda of: columns(dk_out, of, 0, HEAD_DIM)),
+        (lambda to: own_rows(sum_ref.at[1], to, 0), lambda of: columns(dv_out, of, 0, HEAD_DIM)),
+    )
+
+    def exchange(index, step):
+        to = lax.rem(head + step, peers)
+        source, target = routes[index]
+        return pltpu.make_async_remote_copy(
+            src_ref=source(to),
+            dst_ref=target(head),
+            send_sem=send_sem.at[index, step],
+            recv_sem=recv_sem.at[index, step],
+            device_id=(ctx, to),
+            device_id_type=MESH,
+        )
+
+    def keep(index):
+        source, target = routes[index]
+        return pltpu.make_async_copy(source(head), target(head), local_sem.at[index])
+
+    def begin(*indices):
+        for index in indices:
+            keep(index).start()
+            for step in range(1, peers):
+                exchange(index, step).start()
+
+    def arrived(*indices):
+        for index in indices:
+            keep(index).wait()
+            source, target = routes[index]
+            for step in range(1, peers):
+                of = lax.rem(head + peers - step, peers)
+                pltpu.make_async_remote_copy(
+                    src_ref=source(head),
+                    dst_ref=target(of),
+                    send_sem=send_sem.at[index, step],
+                    recv_sem=recv_sem.at[index, step],
+                    device_id=(ctx, of),
+                    device_id_type=MESH,
+                ).wait_recv()
+
+    def halo_copy(run, which):
+        distance, first, end, _ = plan[run]
+        ref = (k_win, v_win)[which]
+        base = halo - distance * rows
+        return pltpu.make_async_remote_copy(
+            src_ref=ref.at[halo + first : halo + end, :],
+            dst_ref=ref.at[base + first : base + end, :],
+            send_sem=halo_send.at[run, which],
+            recv_sem=halo_recv.at[run, which],
+            device_id=(ctx + distance, head),
+            device_id_type=MESH,
+        )
+
+    def back_copy(run, which):
+        distance, first, end, _ = plan[run]
+        base = halo - distance * rows
+        return pltpu.make_async_remote_copy(
+            src_ref=low_ref.at[which, base + first : base + end, :],
+            dst_ref=got_ref.at[which, base + first : base + end, :],
+            send_sem=back_send.at[run, which],
+            recv_sem=back_recv.at[run, which],
+            device_id=(ctx - distance, head),
+            device_id_type=MESH,
+        )
+
+    def for_runs(body, upward):
+        for run, (distance, first, end, senders) in enumerate(plan):
+            if upward:
+                here = is_one_of(ctx, senders, shards)
+            else:
+                here = is_one_of(ctx - distance, senders, shards) & (ctx >= distance)
+
+            @pl.when(here)
+            def _():
+                body(run, distance, first, end)
+
+    begin(0, 1, 2, 3, 4)
+
+    docs = lengths_ref.shape[1]
+    before = lax.broadcasted_iota(jnp.int32, (docs, docs), 1) < lax.broadcasted_iota(
+        jnp.int32, (docs, docs), 0
+    )
+    lengths = lengths_ref[...].astype(jnp.float32)
+    doc_starts = jnp.sum(jnp.where(before, lengths, 0.0), axis=1, keepdims=True)
+    doc_starts = doc_starts - (ctx * rows - halo).astype(jnp.float32)
+    places = lax.broadcasted_iota(jnp.int32, (1, rows), 1).astype(jnp.float32) + float(halo)
+    starts = jnp.max(jnp.where(doc_starts <= places, doc_starts, -1e9), axis=0, keepdims=True)
+    start_ref[...] = starts.astype(jnp.int32)
+    dk_acc[...] = jnp.zeros_like(dk_acc)
+    dv_acc[...] = jnp.zeros_like(dv_acc)
+
+    arrived(0, 1)
+    for_runs(lambda run, *_: [halo_copy(run, which).start() for which in range(2)], True)
+    begin(5, 6)
+
+    reach_tiles = halo // TILE
+    key_offset = lax.broadcasted_iota(jnp.int32, (STEP, TILE), 0)
+    query_offset = lax.broadcasted_iota(jnp.int32, (1, TILE), 1)
+    parts = TILE // part
+
+    def turn(tile, carry):
+        at = pl.ds(pl.multiple_of(tile * TILE, TILE), TILE)
+        kt_ref[:, at] = k_win[at, :].T
+        return carry
+
+    def attend(pair):
+        def query_block(block, carry):
+            q_at = pl.ds(pl.multiple_of(block * TILE, TILE), TILE)
+            end = halo + (block + 1) * TILE
+            tiles = reach_tiles + block + 1 - first_tiles(ctx, block, shards, rows, reach_tiles)
+            count = lax.div(tiles + 1, STEP // TILE)
+            start = start_ref[:, q_at]
+            last = query_offset + (end - TILE)
+            deltas = []
+            for one in pair_heads:
+                which = pair * len(pair_heads) + one
+                cols = slice(which * HEAD_DIM, (which + 1) * HEAD_DIM)
+                q_stack[stacks[one], :] = q_buf[q_at, cols]
+                g_stack[stacks[one], :] = g_buf[q_at, cols]
+                deltas.append(
+                    jnp.concatenate(
+                        [d_buf[block * parts + p, which : which + 1, :] for p in range(parts)],
+                        axis=1,
+                    )
+                )
+
+            def key_rows(step):
+                return pl.multiple_of(end - (step + 1) * STEP, TILE)
+
+            def score_step(step, tops):
+                first = key_rows(step)
+                at = pl.ds(first, STEP)
+                keys = k_win[at, :]
+                place = key_offset + first
+                allowed = (place >= start) & (place <= last)
+                new_tops = []
+                for one in pair_heads:
+                    scores = contract_last(keys, q_stack[stacks[one], :]) * (ATT_SCALE * LOG2E)
+                    scores = jnp.where(allowed, scores, NEG_FILL)
+                    score_ref[at, stacks[one]] = scores
+                    tall = jnp.max(scores.reshape(STEP // 8, 8, TILE), axis=0)
+                    new_tops.append(jnp.maximum(tops[one], tall))
+                return tuple(new_tops)
+
+            none = jnp.full((8, TILE), NEG_FILL, jnp.float32)
+            tops = lax.fori_loop(0, count, score_step, tuple(none for _ in pair_heads))
+            tops = [jnp.max(top, axis=0, keepdims=True) for top in tops]
+
+            def sum_step(step, totals):
+                at = pl.ds(key_rows(step), STEP)
+                new_totals = []
+                for one in pair_heads:
+                    powers = jnp.exp2(score_ref[at, stacks[one]] - tops[one])
+                    tall = jnp.sum(powers.reshape(STEP // 8, 8, TILE), axis=0)
+                    new_totals.append(totals[one] + tall)
+                return tuple(new_totals)
+
+            zero = jnp.zeros((8, TILE), jnp.float32)
+            totals = lax.fori_loop(0, count, sum_step, tuple(zero for _ in pair_heads))
+            log_totals = [
+                tops[one] + jnp.log2(jnp.sum(totals[one], axis=0, keepdims=True))
+                for one in pair_heads
+            ]
+            turned_ref[...] = jnp.zeros_like(turned_ref)
+
+            def grad_step(step, carry):
+                at = pl.ds(key_rows(step), STEP)
+                vals = v_win[at, :]
+                for one in pair_heads:
+                    probs = jnp.exp2(score_ref[at, stacks[one]] - log_totals[one])
+                    grad_probs = contract_last(vals, g_stack[stacks[one], :])
+                    grads = (probs * (grad_probs - deltas[one])).astype(jnp.bfloat16)
+                    probs_ref[:, stacks[one]] = probs.astype(jnp.bfloat16)
+                    grads_ref[:, stacks[one]] = grads
+                dv_acc[at, :] += contract_inner(probs_ref[...], g_stack[...])
+                dk_acc[at, :] += contract_inner(grads_ref[...], q_stack[...])
+                turned_ref[...] += contract_inner(kt_ref[:, at], grads_ref[...])
+                return carry
+
+            lax.fori_loop(0, count, grad_step, 0)
+            for one in pair_heads:
+                which = pair * len(pair_heads) + one
+                dq = turned_ref[:, stacks[one]].T * ATT_SCALE
+                dq_buf[q_at, which * HEAD_DIM : (which + 1) * HEAD_DIM] = dq.astype(jnp.bfloat16)
+            return carry
+
+        lax.fori_loop(0, rows // TILE, query_block, 0)
+
+    arrived(2, 3, 4)
+    for_runs(lambda run, *_: [halo_copy(run, which).wait_recv() for which in range(2)], False)
+    lowest = first_tiles(ctx, 0, shards, rows, reach_tiles) - 1
+    lax.fori_loop(lowest, reach_tiles + rows // TILE, turn, 0)
+    attend(0)
+    begin(7)
+    arrived(5, 6)
+    attend(1)
+
+    def send_back(run, distance, first, end):
+        at = slice(halo - distance * rows + first, halo - distance * rows + end)
+        low_ref[0, at, :] = (dk_acc[at, :] * ATT_SCALE).astype(jnp.bfloat16)
+        low_ref[1, at, :] = dv_acc[at, :].astype(jnp.bfloat16)
+        for which in range(2):
+            back_copy(run, which).start()
+
+    def take_back(run, distance, first, end):
+        got = slice(halo - distance * rows + first, halo - distance * rows + end)
+        for which in range(2):
+            back_copy(run, which).wait_recv()
+            total_ref[which, first:end, :] += got_ref[which, got, :].astype(jnp.float32)
+
+    for_runs(send_back, False)
+    begin(8)
+    total_ref[0] = dk_acc[halo:, :] * ATT_SCALE
+    total_ref[1] = dv_acc[halo:, :]
+    for_runs(take_back, True)
+    sum_ref[...] = total_ref[...].astype(jnp.bfloat16)
+    begin(9, 10)
+    for_runs(lambda run, *_: [halo_copy(run, which).wait_send() for which in range(2)], True)
+    for_runs(lambda run, *_: [back_copy(run, which).wait_send() for which in range(2)], False)
+    arrived(7, 8, 9, 10)
+    for index in range(len(routes)):
+        for step in range(1, peers):
+            exchange(index, step).wait_send()
+
+
+def whole(shards, plan, queries, keys, values, grad_out, delta, doc_lengths):
+    peers = delta.shape[0]
+    part = queries.shape[0]
+    rows = part * peers
+    width = queries.shape[1] // peers
+    window = (REACH + 1) * rows + TILE
+    low, full = jnp.bfloat16, jnp.float32
+    wide = width // 2 // HEAD_DIM * TILE
+    dma = pltpu.SemaphoreType.DMA
+    return pl.pallas_call(
+        functools.partial(whole_kernel, shards, plan),
+        out_shape=(
+            jax.ShapeDtypeStruct(queries.shape, low),
+            jax.ShapeDtypeStruct(keys.shape, low),
+            jax.ShapeDtypeStruct(values.shape, low),
+        ),
+        in_specs=[ANYWHERE] * 4 + [VMEM] * 2,
+        out_specs=(ANYWHERE,) * 3,
+        scratch_shapes=[
+            pltpu.VMEM((rows, width), low),
+            pltpu.VMEM((rows, width), low),
+            pltpu.VMEM((window, HEAD_DIM), low),
+            pltpu.VMEM((window, HEAD_DIM), low),
+            pltpu.VMEM(delta.shape, full),
+            pltpu.VMEM((1, rows), jnp.int32),
+            pltpu.VMEM((HEAD_DIM, window), low),
+            pltpu.VMEM((window, wide), full),
+            pltpu.VMEM((STEP, wide), low),
+            pltpu.VMEM((STEP, wide), low),
+            pltpu.VMEM((wide, HEAD_DIM), low),
+            pltpu.VMEM((wide, HEAD_DIM), low),
+            pltpu.VMEM((HEAD_DIM, wide), full),
+            pltpu.VMEM((window, HEAD_DIM), full),
+            pltpu.VMEM((window, HEAD_DIM), full),
+            pltpu.VMEM((rows, width), low),
+            pltpu.VMEM((2, window - rows, HEAD_DIM), low),
+            pltpu.VMEM((2, window - rows, HEAD_DIM), low),
+            pltpu.VMEM((2, rows, HEAD_DIM), full),
+            pltpu.VMEM((2, rows, HEAD_DIM), low),
+            dma((11, peers)),
+            dma((11, peers)),
+            dma((11,)),
+            dma((len(plan), 2)),
+            dma((len(plan), 2)),
+            dma((len(plan), 2)),
+            dma((len(plan), 2)),
+        ],
+        compiler_params=pltpu.CompilerParams(
+            collective_id=0, has_side_effects=True, vmem_limit_bytes=44 * 1024 * 1024
+        ),
+        name="whole",
+    )(queries, keys, values, grad_out, delta, doc_lengths[None])
 
 
 def on_device(queries, keys, values, grad_out, delta, doc_lengths):
@@ -539,29 +937,22 @@
             jnp.where(doc_starts[:, None] <= places[None, :], doc_starts[:, None], 0), axis=0
         )
 
-    base = lax.axis_index("ctx") * rows
-    starts = start_at(base + jnp.arange(rows, dtype=jnp.int32)) - (base - REACH * rows - TILE)
-    first_row = starts[::TILE]
-    edges = jnp.arange(shards, dtype=jnp.int32) * rows
-    reach = jnp.array(halo_reach(shards, rows), jnp.int32)
-    fits = jnp.all(start_at(edges) >= edges - reach)
-
-    def run(short, *operands):
-        plan = halo_plan(shards, rows, short)
-        q, k, v, g, d = gather(shards, plan, short, *operands)
-        dq, dk, dv = attention(first_row, q, g, k, v, d, starts[None])
-        return scatter(shards, plan, short, peers, dq, dk, dv)
-
-    return lax.cond(
-        fits,
-        functools.partial(run, True),
-        functools.partial(run, False),
-        queries,
-        keys,
-        values,
-        grad_out,
-        delta,
-    )
+    blocks = np.arange(shards * rows // TILE)
+    lowest = jnp.asarray(short_reach(blocks, shards, rows), jnp.int32)
+    fits = jnp.all(start_at(jnp.asarray(blocks * TILE, jnp.int32)) >= lowest)
+
+    def in_one(*operands):
+        return whole(shards, halo_plan(shards, rows, True), *operands, doc_lengths)
+
+    def in_three(*operands):
+        plan = halo_plan(shards, rows, False)
+        base = lax.axis_index("ctx") * rows
+        starts = start_at(base + jnp.arange(rows, dtype=jnp.int32)) - (base - REACH * rows - TILE)
+        q, k, v, g, d = gather(shards, plan, *operands)
+        dq, dk, dv = attention(starts[::TILE], q, g, k, v, d, starts[None])
+        return scatter(shards, plan, peers, dq, dk, dv)
+
+    return lax.cond(fits, in_one, in_three, queries, keys, values, grad_out, delta)
 
 
 def solution(mesh):

time: 120 us -> 159 us (1.32)
  the two profiles are of different devices: /device:TPU:16 before, /device:TPU:280 now
where the time goes in v4:
time: 159 us; the launch traced here: 158 us
  Pallas kernels  152 us (96%)
  local copies, waits for them, and re-layouts  2.47 us (2%)
  other arithmetic  2.46 us (2%)
    pallas_call x1, Pallas kernels, scatter(): pl.pallas_call(functools.partial(scatter_kernel, shards, plan), out_shape...  77.2 us
    pallas_call x1, Pallas kernels, gather(): pl.pallas_call(functools.partial(gather_kernel, shards, plan), out_shape=...  54.5 us
    pallas_call x1, Pallas kernels, attention(): pl.pallas_call(attention_kernel, out_shape=(jax.ShapeDtypeStruct(q.shape,...  20.3 us

profile of v4, /device:TPU:280, one launch (start us, length us, event | category | flops | bytes accessed | tf_op | source)
XLA Modules:
  0.0 158.3 jit_solution(15275855939507245901)
XLA Ops:
  0.6 0.8 select_reduce_fusion.2
  1.4 0.1 select_reduce_fusion.1
  1.5 1.3 compare_reduce_fusion
  3.5 152.4 %conditional.1 = ((bf16[128,4096]{1,0:T(8,128)(2,1)S(1)}, bf16[128,1024]{1,0:T(8,128)(2,1)S(1)}, bf16[128,1024]{1,0:T(8,128)(2,1)S(1)})) conditional(s32[]{:T(128)} %convert_element_type.3, (s32[256]{0:T(256)S(1)}, bf16[128,4096]{1,0:T(8,128)(2,1)}, bf16[128,1024]{1,0:T(8,128)(2,1)}, bf16[128,1024]{1,0:T(8,128)(2,1)}, bf16[128,4096]{1,0:T(8,128)(2,1)}, ...), branch_computations={%region_3.5_spmd, %region_5.6_spmd} | conditional | flops 787461 | bytes 21608 | solution.py:955
  3.6 0.2 select_reduce_fusion
  3.8 0.1 slice.2.first_row
  3.9 54.5 %gather.1 = (bf16[1024,512]{1,0:T(8,128)(2,1)S(1)}, bf16[3328,128]{1,0:T(8,128)(2,1)S(1)}, bf16[3328,128]{1,0:T(8,128)(2,1)S(1)}, bf16[1024,512]{1,0:T(8,128)(2,1)S(1)}, f32[8,4,128]{2,1,0:T(4,128)S(1)}) custom-call(bf16[128,4096]{1,0:T(8,128)(2,1)} %get-tuple-element.25.q_in, bf16[128,1024]{1,0:T(8,128)(2,1)} %get-tuple-element.26.k_in, ...), custom_call_target="tpu_custom_call" | custom-call | tf_op jit(solution)/shard_map/cond/branch_0_fun/gather/pallas_call | solution.py:215
  58.4 20.3 %attention.1 = (bf16[1024,512]{1,0:T(8,128)(2,1)S(1)}, f32[3328,128]{1,0:T(8,128)S(1)}, f32[3328,128]{1,0:T(8,128)S(1)}) custom-call(s32[4]{0:T(128)S(1)} %slice.2.first_row, bf16[1024,512]{1,0:T(8,128)(2,1)S(1)} %get-tuple-element.30.q_ref, bf16[1024,512]{1,0:T(8,128)(2,1)S(1)} %get-tuple-element.31.g_ref, bf16[3328,128]{1,0:T(8,128)(2,1)S(1)} %get-tuple-element.32.k_ref, ...), custom_call_target="tpu_custom_call" | custom-call | tf_op jit(solution)/shard_map/cond/branch_0_fun/attention/pallas_call | solution.py:356
  78.8 77.2 %scatter.1 = (bf16[128,4096]{1,0:T(8,128)(2,1)S(1)}, bf16[128,1024]{1,0:T(8,128)(2,1)S(1)}, bf16[128,1024]{1,0:T(8,128)(2,1)S(1)}) custom-call(bf16[1024,512]{1,0:T(8,128)(2,1)S(1)} %get-tuple-element.35.dq_in, f32[3328,128]{1,0:T(8,128)S(1)} %get-tuple-element.36.dk_in, f32[3328,128]{1,0:T(8,128)S(1)} %get-tuple-element.37.dv_in), custom_call_target="tpu_custom_call" | custom-call | tf_op jit(solution)/shard_map/cond/branch_0_fun/scatter/pallas_call | solution.py:503
  156.0 1.0 copy.26
  156.9 0.7 copy.27
  157.6 0.7 copy.28
  (3 shorter events, 0.0 us)

commit v5 on v4

--- a/solution.py
+++ b/solution.py
@@ -43,7 +43,7 @@
 
 def short_reach(blocks, shards, rows):
     shard = blocks * TILE // rows
-    reach = (blocks - 1) * TILE
+    reach = np.where(shard == 0, 0, (blocks - 1) * TILE)
     for first in long_firsts(shards):
         opening = first * rows + rows // 2
         for other in (first + 1, first + 2):
@@ -536,6 +536,7 @@
     second = is_one_of(ctx, tuple(first + 1 for first in firsts), shards)
     third = is_one_of(ctx, tuple(first + 2 for first in firsts), shards)
     low = jnp.where(second, jnp.minimum(reach_tiles - half, reach_tiles + block - 1), reach_tiles + block - 1)
+    low = jnp.where(ctx == 0, reach_tiles, low)
     return jnp.where(third, reach_tiles - own - half, low)
 
 

time: 159 us -> 114 us (0.72)
  the two profiles are of different devices: /device:TPU:280 before, /device:TPU:8 now
where the time goes in v5:
time: 114 us
  Pallas kernels  108 us (95%)
  local copies, waits for them, and re-layouts  2.38 us (2%)
  other arithmetic  2.24 us (2%)
  between operations  1.3 us (1%)
    pallas_call x1, Pallas kernels, whole(): pl.pallas_call(functools.partial(whole_kernel, shards, plan), out_shape=(...  108 us
    unnamed x3, local copies, waits for them, and re-layouts  2.38 us

profile of v5, /device:TPU:8, one launch (start us, length us, event | category | flops | bytes accessed | tf_op | source)
XLA Modules:
  0.0 113.8 jit_solution(4389796880117341292)
XLA Ops:
  0.6 0.8 select_reduce_fusion.2
  1.4 0.1 select_reduce_fusion.1
  1.5 1.3 %compare_reduce_fusion = pred[]{:T(512)} fusion(s32[256]{0:T(256)S(1)} %select_reduce_fusion.1, s32[256]{0:T(256)} %constant.29.clone), kind=kLoop, calls=%fused_computation.6 | loop fusion | flops 511 | bytes 2049 | tf_op jit(solution)/shard_map/reduce_and | solution.py:943
  3.5 107.9 %conditional.1 = ((bf16[128,4096]{1,0:T(8,128)(2,1)S(1)}, bf16[128,1024]{1,0:T(8,128)(2,1)S(1)}, bf16[128,1024]{1,0:T(8,128)(2,1)S(1)})) conditional(s32[]{:T(128)} %convert_element_type.3, (s32[256]{0:T(256)S(1)}, bf16[128,4096]{1,0:T(8,128)(2,1)}, bf16[128,1024]{1,0:T(8,128)(2,1)}, bf16[128,1024]{1,0:T(8,128)(2,1)}, bf16[128,4096]{1,0:T(8,128)(2,1)}, ...), branch_computations={%region_3.5_spmd, %region_5.6_spmd} | conditional | flops 787461 | bytes 21608 | solution.py:956
  3.5 107.9 %whole.1 = (bf16[128,4096]{1,0:T(8,128)(2,1)S(1)}, bf16[128,1024]{1,0:T(8,128)(2,1)S(1)}, bf16[128,1024]{1,0:T(8,128)(2,1)S(1)}) custom-call(bf16[128,4096]{1,0:T(8,128)(2,1)} %get-tuple-element.38.q_in, bf16[128,1024]{1,0:T(8,128)(2,1)} %get-tuple-element.39.k_in, bf16[128,1024]{1,0:T(8,128)(2,1)} %get-tuple-element.40.v_in, ...), custom_call_target="tpu_custom_call" | custom-call | tf_op jit(solution)/shard_map/cond/branch_1_fun/whole/pallas_call | solution.py:884
  111.4 1.0 copy.26
  112.4 0.7 copy.27
  113.1 0.7 copy.28
  (1 shorter events, 0.0 us)

commit v6 on v5

--- a/solution.py
+++ b/solution.py
@@ -2,7 +2,6 @@
 
 import jax
 import jax.numpy as jnp
-import numpy as np
 from jax import lax
 from jax.experimental import pallas as pl
 from jax.experimental.pallas import tpu as pltpu
@@ -11,6 +10,7 @@
 HEAD_DIM = 128
 TILE = 256
 STEP = 512
+BLOCK = 512
 REACH = 2
 NEG_FILL = -1e30
 ATT_SCALE = HEAD_DIM ** (-0.5)
@@ -42,12 +42,12 @@
 
 
 def short_reach(blocks, shards, rows):
-    shard = blocks * TILE // rows
-    reach = np.where(shard == 0, 0, (blocks - 1) * TILE)
+    shard = blocks // (rows // BLOCK)
+    reach = jnp.where(shard == 0, 0, blocks * BLOCK - TILE)
     for first in long_firsts(shards):
         opening = first * rows + rows // 2
-        for other in (first + 1, first + 2):
-            reach = np.where(shard == other, np.minimum(reach, opening), reach)
+        holds = (shard == first + 1) | (shard == first + 2)
+        reach = jnp.where(holds, jnp.minimum(reach, opening), reach)
     return reach
 
 
@@ -535,8 +535,9 @@
     firsts = long_firsts(shards)
     second = is_one_of(ctx, tuple(first + 1 for first in firsts), shards)
     third = is_one_of(ctx, tuple(first + 2 for first in firsts), shards)
-    low = jnp.where(second, jnp.minimum(reach_tiles - half, reach_tiles + block - 1), reach_tiles + block - 1)
+    low = reach_tiles + block * (BLOCK // TILE) - 1
     low = jnp.where(ctx == 0, reach_tiles, low)
+    low = jnp.where(second, reach_tiles - half, low)
     return jnp.where(third, reach_tiles - own - half, low)
 
 
@@ -587,7 +588,7 @@
     halo = k_win.shape[0] - rows
     half_width = width // 2
     pair_heads = range(half_width // HEAD_DIM)
-    stacks = [slice(one * TILE, (one + 1) * TILE) for one in pair_heads]
+    stacks = [slice(one * BLOCK, (one + 1) * BLOCK) for one in pair_heads]
     k_win[:halo, :] = jnp.zeros((halo, HEAD_DIM), k_win.dtype)
     v_win[:halo, :] = jnp.zeros((halo, HEAD_DIM), v_win.dtype)
 
@@ -743,9 +744,14 @@
     begin(5, 6)
 
     reach_tiles = halo // TILE
-    key_offset = lax.broadcasted_iota(jnp.int32, (STEP, TILE), 0)
-    query_offset = lax.broadcasted_iota(jnp.int32, (1, TILE), 1)
-    parts = TILE // part
+    key_offset = lax.broadcasted_iota(jnp.int32, (STEP, BLOCK), 0)
+    query_offset = lax.broadcasted_iota(jnp.int32, (1, BLOCK), 1)
+    parts = BLOCK // part
+
+    def block_steps(block):
+        low = first_tiles(ctx, block, shards, rows, reach_tiles)
+        tiles = reach_tiles + (block + 1) * (BLOCK // TILE) - low
+        return lax.div(tiles + STEP // TILE - 1, STEP // TILE)
 
     def turn(tile, carry):
         at = pl.ds(pl.multiple_of(tile * TILE, TILE), TILE)
@@ -754,12 +760,11 @@
 
     def attend(pair):
         def query_block(block, carry):
-            q_at = pl.ds(pl.multiple_of(block * TILE, TILE), TILE)
-            end = halo + (block + 1) * TILE
-            tiles = reach_tiles + block + 1 - first_tiles(ctx, block, shards, rows, reach_tiles)
-            count = lax.div(tiles + 1, STEP // TILE)
+            q_at = pl.ds(pl.multiple_of(block * BLOCK, BLOCK), BLOCK)
+            end = halo + (block + 1) * BLOCK
+            count = block_steps(block)
             start = start_ref[:, q_at]
-            last = query_offset + (end - TILE)
+            last = query_offset + (end - BLOCK)
             deltas = []
             for one in pair_heads:
                 which = pair * len(pair_heads) + one
@@ -787,11 +792,11 @@
                     scores = contract_last(keys, q_stack[stacks[one], :]) * (ATT_SCALE * LOG2E)
                     scores = jnp.where(allowed, scores, NEG_FILL)
                     score_ref[at, stacks[one]] = scores
-                    tall = jnp.max(scores.reshape(STEP // 8, 8, TILE), axis=0)
+                    tall = jnp.max(scores.reshape(STEP // 8, 8, BLOCK), axis=0)
                     new_tops.append(jnp.maximum(tops[one], tall))
                 return tuple(new_tops)
 
-            none = jnp.full((8, TILE), NEG_FILL, jnp.float32)
+            none = jnp.full((8, BLOCK), NEG_FILL, jnp.float32)
             tops = lax.fori_loop(0, count, score_step, tuple(none for _ in pair_heads))
             tops = [jnp.max(top, axis=0, keepdims=True) for top in tops]
 
@@ -800,11 +805,11 @@
                 new_totals = []
                 for one in pair_heads:
                     powers = jnp.exp2(score_ref[at, stacks[one]] - tops[one])
-                    tall = jnp.sum(powers.reshape(STEP // 8, 8, TILE), axis=0)
+                    tall = jnp.sum(powers.reshape(STEP // 8, 8, BLOCK), axis=0)
                     new_totals.append(totals[one] + tall)
                 return tuple(new_totals)
 
-            zero = jnp.zeros((8, TILE), jnp.float32)
+            zero = jnp.zeros((8, BLOCK), jnp.float32)
             totals = lax.fori_loop(0, count, sum_step, tuple(zero for _ in pair_heads))
             log_totals = [
                 tops[one] + jnp.log2(jnp.sum(totals[one], axis=0, keepdims=True))
@@ -833,11 +838,11 @@
                 dq_buf[q_at, which * HEAD_DIM : (which + 1) * HEAD_DIM] = dq.astype(jnp.bfloat16)
             return carry
 
-        lax.fori_loop(0, rows // TILE, query_block, 0)
+        lax.fori_loop(0, rows // BLOCK, query_block, 0)
 
     arrived(2, 3, 4)
     for_runs(lambda run, *_: [halo_copy(run, which).wait_recv() for which in range(2)], False)
-    lowest = first_tiles(ctx, 0, shards, rows, reach_tiles) - 1
+    lowest = reach_tiles + BLOCK // TILE - block_steps(0) * (STEP // TILE)
     lax.fori_loop(lowest, reach_tiles + rows // TILE, turn, 0)
     attend(0)
     begin(7)
@@ -879,7 +884,7 @@
     width = queries.shape[1] // peers
     window = (REACH + 1) * rows + TILE
     low, full = jnp.bfloat16, jnp.float32
-    wide = width // 2 // HEAD_DIM * TILE
+    wide = width // 2 // HEAD_DIM * BLOCK
     dma = pltpu.SemaphoreType.DMA
     return pl.pallas_call(
         functools.partial(whole_kernel, shards, plan),
@@ -920,10 +925,33 @@
             dma((len(plan), 2)),
         ],
         compiler_params=pltpu.CompilerParams(
-            collective_id=0, has_side_effects=True, vmem_limit_bytes=44 * 1024 * 1024
+            collective_id=0, has_side_effects=True, vmem_limit_bytes=48 * 1024 * 1024
         ),
         name="whole",
     )(queries, keys, values, grad_out, delta, doc_lengths[None])
+
+
+def settle_kernel(*refs):
+    count = len(refs) // 2
+    sems = refs[-1]
+    copies = [
+        pltpu.make_async_copy(refs[one], refs[count + one], sems.at[one]) for one in range(count)
+    ]
+    for copy in copies:
+        copy.start()
+    for copy in copies:
+        copy.wait()
+
+
+def settled(*arrays):
+    return pl.pallas_call(
+        settle_kernel,
+        out_shape=tuple(jax.ShapeDtypeStruct(a.shape, a.dtype) for a in arrays),
+        in_specs=[ANYWHERE] * len(arrays),
+        out_specs=(ANYWHERE,) * len(arrays),
+        scratch_shapes=[pltpu.SemaphoreType.DMA((len(arrays),))],
+        name="settle",
+    )(*arrays)
 
 
 def on_device(queries, keys, values, grad_out, delta, doc_lengths):
@@ -938,9 +966,8 @@
             jnp.where(doc_starts[:, None] <= places[None, :], doc_starts[:, None], 0), axis=0
         )
 
-    blocks = np.arange(shards * rows // TILE)
-    lowest = jnp.asarray(short_reach(blocks, shards, rows), jnp.int32)
-    fits = jnp.all(start_at(jnp.asarray(blocks * TILE, jnp.int32)) >= lowest)
+    last_block = lax.div(doc_starts + doc_lengths - 1, jnp.int32(BLOCK))
+    fits = jnp.all(doc_starts >= short_reach(last_block, shards, rows))
 
     def in_one(*operands):
         return whole(shards, halo_plan(shards, rows, True), *operands, doc_lengths)
@@ -953,7 +980,7 @@
         dq, dk, dv = attention(starts[::TILE], q, g, k, v, d, starts[None])
         return scatter(shards, plan, peers, dq, dk, dv)
 
-    return lax.cond(fits, in_one, in_three, queries, keys, values, grad_out, delta)
+    return settled(*lax.cond(fits, in_one, in_three, queries, keys, values, grad_out, delta))
 
 
 def solution(mesh):

time: 114 us -> 108 us (0.947)
  Pallas kernels: 108 us -> 105 us
  local copies, waits for them, and re-layouts: 2.38 us -> 0 us
    pallas_call x1, Pallas kernels: 108 us -> 103 us  [whole(): pl.pallas_call(functools.partial(whole_kernel, shards, plan), out_shape=(...]
    unnamed x3 -> x0, local copies, waits for them, and re-layouts: 2.38 us -> none
    pallas_call x0 -> x1, Pallas kernels: none -> 1.16 us  [settled(): pl.pallas_call(settle_kernel, out_shape=tuple((jax.ShapeDtypeStruct(a.sha...]
where the time goes in v6:
time: 108 us
  Pallas kernels  105 us (97%)
  other arithmetic  2.14 us (2%)
  between operations  1.29 us (1%)
    pallas_call x1, Pallas kernels, whole(): pl.pallas_call(functools.partial(whole_kernel, shards, plan), out_shape=(...  103 us

profile of v6, /device:TPU:8, one launch (start us, length us, event | category | flops | bytes accessed | tf_op | source)
XLA Modules:
  0.0 108.0 jit_solution(15369441093980297324)
XLA Ops:
  0.6 0.8 select_reduce_fusion.1
  1.4 1.3 %compare_reduce_fusion = pred[]{:T(512)} fusion(s32[256]{0:T(256)S(1)} %select_reduce_fusion.1, s32[256]{0:T(256)} %param.13), kind=kLoop, calls=%fused_computation.7 | loop fusion | flops 13823 | bytes 2049 | tf_op jit(solution)/shard_map/reduce_and | solution.py:970
  3.4 103.4 %conditional.1 = ((bf16[128,4096]{1,0:T(8,128)(2,1)S(1)}, bf16[128,1024]{1,0:T(8,128)(2,1)S(1)}, bf16[128,1024]{1,0:T(8,128)(2,1)S(1)})) conditional(s32[]{:T(128)} %convert_element_type.3, (s32[256]{0:T(256)S(1)}, bf16[128,4096]{1,0:T(8,128)(2,1)}, bf16[128,1024]{1,0:T(8,128)(2,1)}, bf16[128,1024]{1,0:T(8,128)(2,1)}, bf16[128,4096]{1,0:T(8,128)(2,1)}, ...), branch_computations={%region_2.4_spmd, %region_4.5_spmd} | conditional | flops 787461 | bytes 21608 | solution.py:983
  3.4 103.4 %whole.1 = (bf16[128,4096]{1,0:T(8,128)(2,1)S(1)}, bf16[128,1024]{1,0:T(8,128)(2,1)S(1)}, bf16[128,1024]{1,0:T(8,128)(2,1)S(1)}) custom-call(bf16[128,4096]{1,0:T(8,128)(2,1)} %get-tuple-element.38.q_in, bf16[128,1024]{1,0:T(8,128)(2,1)} %get-tuple-element.39.k_in, bf16[128,1024]{1,0:T(8,128)(2,1)} %get-tuple-element.40.v_in, ...), custom_call_target="tpu_custom_call" | custom-call | tf_op jit(solution)/shard_map/cond/branch_1_fun/whole/pallas_call | solution.py:889
  106.9 1.2 %settle.1 = (bf16[128,4096]{1,0:T(8,128)(2,1)}, bf16[128,1024]{1,0:T(8,128)(2,1)}, bf16[128,1024]{1,0:T(8,128)(2,1)}) custom-call(bf16[128,4096]{1,0:T(8,128)(2,1)S(1)} %get-tuple-element.50.refs_0_, bf16[128,1024]{1,0:T(8,128)(2,1)S(1)} %get-tuple-element.51.refs_1_, bf16[128,1024]{1,0:T(8,128)(2,1)S(1)} %get-tuple-element.52.refs_2_), custom_call_target="tpu_custom_call" | custom-call | tf_op jit(solution)/shard_map/settle/pallas_call | solution.py:947

commit v7 on v6

--- a/solution.py
+++ b/solution.py
@@ -11,6 +11,7 @@
 TILE = 256
 STEP = 512
 BLOCK = 512
+HOPS = ((2, 1), (2, 0), (1, 1), (3, 1), (0, 1), (1, 0), (3, 0))
 REACH = 2
 NEG_FILL = -1e30
 ATT_SCALE = HEAD_DIM ** (-0.5)
@@ -565,6 +566,8 @@
     grads_ref,
     q_stack,
     g_stack,
+    delta_ref,
+    log_ref,
     turned_ref,
     dk_acc,
     dv_acc,
@@ -614,6 +617,12 @@
     around = jnp.minimum(shards - 1 - ctx, REACH) + jnp.minimum(ctx, REACH)
     pl.semaphore_wait(barrier, peers - 1 + around)
 
+    def partner(step, sign):
+        along, across = HOPS[step - 1]
+        line = peers // 2
+        moved = lax.rem(lax.div(head, 2) + (along if sign > 0 else line - along), line)
+        return moved * 2 + lax.rem(head + across, 2)
+
     def columns(ref, owner, offset, size):
         stride = ref.shape[1] // peers
         return ref.at[:, pl.ds(pl.multiple_of(owner * stride + offset, size), size)]
@@ -652,7 +661,7 @@
     )
 
     def exchange(index, step):
-        to = lax.rem(head + step, peers)
+        to = partner(step, 1)
         source, target = routes[index]
         return pltpu.make_async_remote_copy(
             src_ref=source(to),
@@ -673,12 +682,25 @@
             for step in range(1, peers):
                 exchange(index, step).start()
 
+    def begin_block(index, block):
+        per_block = BLOCK // part
+
+        @pl.when(lax.div(head, per_block) == block)
+        def _():
+            keep(index).start()
+
+        for step in range(1, peers):
+
+            @pl.when(lax.div(partner(step, 1), per_block) == block)
+            def _():
+                exchange(index, step).start()
+
     def arrived(*indices):
         for index in indices:
             keep(index).wait()
             source, target = routes[index]
             for step in range(1, peers):
-                of = lax.rem(head + peers - step, peers)
+                of = partner(step, -1)
                 pltpu.make_async_remote_copy(
                     src_ref=source(head),
                     dst_ref=target(of),
@@ -724,7 +746,7 @@
             def _():
                 body(run, distance, first, end)
 
-    begin(0, 1, 2, 3, 4)
+    begin(0, 1, 3, 2, 4)
 
     docs = lengths_ref.shape[1]
     before = lax.broadcasted_iota(jnp.int32, (docs, docs), 1) < lax.broadcasted_iota(
@@ -739,8 +761,9 @@
     dk_acc[...] = jnp.zeros_like(dk_acc)
     dv_acc[...] = jnp.zeros_like(dv_acc)
 
-    arrived(0, 1)
-    for_runs(lambda run, *_: [halo_copy(run, which).start() for which in range(2)], True)
+    for which in range(2):
+        arrived(which)
+        for_runs(lambda run, *_: halo_copy(run, which).start(), True)
     begin(5, 6)
 
     reach_tiles = halo // TILE
@@ -758,40 +781,34 @@
         kt_ref[:, at] = k_win[at, :].T
         return carry
 
-    def attend(pair):
+    def key_rows(block, step):
+        return pl.multiple_of(halo + (block + 1) * BLOCK - (step + 1) * STEP, TILE)
+
+    def query_rows(block):
+        return pl.ds(pl.multiple_of(block * BLOCK, BLOCK), BLOCK)
+
+    def attend_sums(pair):
         def query_block(block, carry):
-            q_at = pl.ds(pl.multiple_of(block * BLOCK, BLOCK), BLOCK)
-            end = halo + (block + 1) * BLOCK
+            q_at = query_rows(block)
             count = block_steps(block)
             start = start_ref[:, q_at]
-            last = query_offset + (end - BLOCK)
-            deltas = []
+            last = query_offset + (halo + block * BLOCK)
             for one in pair_heads:
                 which = pair * len(pair_heads) + one
                 cols = slice(which * HEAD_DIM, (which + 1) * HEAD_DIM)
-                q_stack[stacks[one], :] = q_buf[q_at, cols]
-                g_stack[stacks[one], :] = g_buf[q_at, cols]
-                deltas.append(
-                    jnp.concatenate(
-                        [d_buf[block * parts + p, which : which + 1, :] for p in range(parts)],
-                        axis=1,
-                    )
-                )
-
-            def key_rows(step):
-                return pl.multiple_of(end - (step + 1) * STEP, TILE)
+                q_stack[block, stacks[one], :] = q_buf[q_at, cols]
 
             def score_step(step, tops):
-                first = key_rows(step)
+                first = key_rows(block, step)
                 at = pl.ds(first, STEP)
                 keys = k_win[at, :]
                 place = key_offset + first
                 allowed = (place >= start) & (place <= last)
                 new_tops = []
                 for one in pair_heads:
-                    scores = contract_last(keys, q_stack[stacks[one], :]) * (ATT_SCALE * LOG2E)
-                    scores = jnp.where(allowed, scores, NEG_FILL)
-                    score_ref[at, stacks[one]] = scores
+                    scores = contract_last(keys, q_stack[block, stacks[one], :])
+                    scores = jnp.where(allowed, scores * (ATT_SCALE * LOG2E), NEG_FILL)
+                    score_ref[block, at, stacks[one]] = scores
                     tall = jnp.max(scores.reshape(STEP // 8, 8, BLOCK), axis=0)
                     new_tops.append(jnp.maximum(tops[one], tall))
                 return tuple(new_tops)
@@ -801,74 +818,107 @@
             tops = [jnp.max(top, axis=0, keepdims=True) for top in tops]
 
             def sum_step(step, totals):
-                at = pl.ds(key_rows(step), STEP)
+                at = pl.ds(key_rows(block, step), STEP)
                 new_totals = []
                 for one in pair_heads:
-                    powers = jnp.exp2(score_ref[at, stacks[one]] - tops[one])
+                    powers = jnp.exp2(score_ref[block, at, stacks[one]] - tops[one])
                     tall = jnp.sum(powers.reshape(STEP // 8, 8, BLOCK), axis=0)
                     new_totals.append(totals[one] + tall)
                 return tuple(new_totals)
 
             zero = jnp.zeros((8, BLOCK), jnp.float32)
             totals = lax.fori_loop(0, count, sum_step, tuple(zero for _ in pair_heads))
-            log_totals = [
-                tops[one] + jnp.log2(jnp.sum(totals[one], axis=0, keepdims=True))
-                for one in pair_heads
-            ]
-            turned_ref[...] = jnp.zeros_like(turned_ref)
-
-            def grad_step(step, carry):
-                at = pl.ds(key_rows(step), STEP)
-                vals = v_win[at, :]
-                for one in pair_heads:
-                    probs = jnp.exp2(score_ref[at, stacks[one]] - log_totals[one])
-                    grad_probs = contract_last(vals, g_stack[stacks[one], :])
-                    grads = (probs * (grad_probs - deltas[one])).astype(jnp.bfloat16)
-                    probs_ref[:, stacks[one]] = probs.astype(jnp.bfloat16)
-                    grads_ref[:, stacks[one]] = grads
-                dv_acc[at, :] += contract_inner(probs_ref[...], g_stack[...])
-                dk_acc[at, :] += contract_inner(grads_ref[...], q_stack[...])
-                turned_ref[...] += contract_inner(kt_ref[:, at], grads_ref[...])
-                return carry
-
-            lax.fori_loop(0, count, grad_step, 0)
+            for one in pair_heads:
+                total = jnp.sum(totals[one], axis=0, keepdims=True)
+                log_ref[block, :, stacks[one]] = tops[one] + jnp.log2(total)
+            turned_ref[block] = jnp.zeros(turned_ref.shape[1:], jnp.float32)
+            return carry
+
+        lax.fori_loop(0, rows // BLOCK, query_block, 0)
+
+    def grad_steps(block, first, end):
+        def grad_step(step, carry):
+            at = pl.ds(key_rows(block, step), STEP)
+            vals = v_win[at, :]
+            for one in pair_heads:
+                logs = log_ref[block, :, stacks[one]]
+                probs = jnp.exp2(score_ref[block, at, stacks[one]] - logs)
+                grad_probs = contract_last(vals, g_stack[block, stacks[one], :])
+                grads = probs * (grad_probs - delta_ref[block, :, stacks[one]])
+                probs_ref[:, stacks[one]] = probs.astype(jnp.bfloat16)
+                grads_ref[:, stacks[one]] = grads.astype(jnp.bfloat16)
+            dv_acc[at, :] += contract_inner(probs_ref[...], g_stack[block])
+            dk_acc[at, :] += contract_inner(grads_ref[...], q_stack[block])
+            turned_ref[block] += contract_inner(kt_ref[:, at], grads_ref[...])
+            return carry
+
+        lax.fori_loop(first, end, grad_step, 0)
+
+    def attend_halo(pair):
+        def query_block(block, carry):
             for one in pair_heads:
                 which = pair * len(pair_heads) + one
-                dq = turned_ref[:, stacks[one]].T * ATT_SCALE
-                dq_buf[q_at, which * HEAD_DIM : (which + 1) * HEAD_DIM] = dq.astype(jnp.bfloat16)
+                cols = slice(which * HEAD_DIM, (which + 1) * HEAD_DIM)
+                g_stack[block, stacks[one], :] = g_buf[query_rows(block), cols]
+                delta_ref[block, :, stacks[one]] = jnp.concatenate(
+                    [d_buf[block * parts + p, which : which + 1, :] for p in range(parts)], axis=1
+                )
+            grad_steps(block, block + 1, block_steps(block))
             return carry
 
         lax.fori_loop(0, rows // BLOCK, query_block, 0)
 
-    arrived(2, 3, 4)
-    for_runs(lambda run, *_: [halo_copy(run, which).wait_recv() for which in range(2)], False)
+    def attend_own(pair, index):
+        def query_block(block, carry):
+            grad_steps(block, 0, jnp.minimum(block + 1, block_steps(block)))
+            for one in pair_heads:
+                which = pair * len(pair_heads) + one
+                dq = turned_ref[block, :, stacks[one]].T * ATT_SCALE
+                cols = slice(which * HEAD_DIM, (which + 1) * HEAD_DIM)
+                dq_buf[query_rows(block), cols] = dq.astype(jnp.bfloat16)
+            begin_block(index, block)
+            return carry
+
+        lax.fori_loop(0, rows // BLOCK, query_block, 0)
+
+    arrived(3)
+    for_runs(lambda run, *_: halo_copy(run, 0).wait_recv(), False)
+    attend_sums(0)
+    arrived(2, 4)
+    for_runs(lambda run, *_: halo_copy(run, 1).wait_recv(), False)
     lowest = reach_tiles + BLOCK // TILE - block_steps(0) * (STEP // TILE)
     lax.fori_loop(lowest, reach_tiles + rows // TILE, turn, 0)
-    attend(0)
-    begin(7)
-    arrived(5, 6)
-    attend(1)
-
-    def send_back(run, distance, first, end):
-        at = slice(halo - distance * rows + first, halo - distance * rows + end)
-        low_ref[0, at, :] = (dk_acc[at, :] * ATT_SCALE).astype(jnp.bfloat16)
-        low_ref[1, at, :] = dv_acc[at, :].astype(jnp.bfloat16)
-        for which in range(2):
+    attend_halo(0)
+    attend_own(0, 7)
+    arrived(5)
+    attend_sums(1)
+    arrived(6)
+    attend_halo(1)
+
+    for which in range(2):
+
+        def send_back(run, distance, first, end):
+            at = slice(halo - distance * rows + first, halo - distance * rows + end)
+            part_sum = dv_acc[at, :] if which else dk_acc[at, :] * ATT_SCALE
+            low_ref[which, at, :] = part_sum.astype(jnp.bfloat16)
             back_copy(run, which).start()
 
-    def take_back(run, distance, first, end):
-        got = slice(halo - distance * rows + first, halo - distance * rows + end)
-        for which in range(2):
+        for_runs(send_back, False)
+
+    attend_own(1, 8)
+    total_ref[0] = dk_acc[halo:, :] * ATT_SCALE
+    total_ref[1] = dv_acc[halo:, :]
+    for which in range(2):
+
+        def take_back(run, distance, first, end):
+            got = slice(halo - distance * rows + first, halo - distance * rows + end)
             back_copy(run, which).wait_recv()
             total_ref[which, first:end, :] += got_ref[which, got, :].astype(jnp.float32)
 
-    for_runs(send_back, False)
-    begin(8)
-    total_ref[0] = dk_acc[halo:, :] * ATT_SCALE
-    total_ref[1] = dv_acc[halo:, :]
-    for_runs(take_back, True)
-    sum_ref[...] = total_ref[...].astype(jnp.bfloat16)
-    begin(9, 10)
+        for_runs(take_back, True)
+        sum_ref[which] = total_ref[which].astype(jnp.bfloat16)
+        begin(9 + which)
+
     for_runs(lambda run, *_: [halo_copy(run, which).wait_send() for which in range(2)], True)
     for_runs(lambda run, *_: [back_copy(run, which).wait_send() for which in range(2)], False)
     arrived(7, 8, 9, 10)
@@ -885,6 +935,7 @@
     window = (REACH + 1) * rows + TILE
     low, full = jnp.bfloat16, jnp.float32
     wide = width // 2 // HEAD_DIM * BLOCK
+    blocks = rows // BLOCK
     dma = pltpu.SemaphoreType.DMA
     return pl.pallas_call(
         functools.partial(whole_kernel, shards, plan),
@@ -903,12 +954,14 @@
             pltpu.VMEM(delta.shape, full),
             pltpu.VMEM((1, rows), jnp.int32),
             pltpu.VMEM((HEAD_DIM, window), low),
-            pltpu.VMEM((window, wide), full),
+            pltpu.VMEM((blocks, window, wide), full),
             pltpu.VMEM((STEP, wide), low),
             pltpu.VMEM((STEP, wide), low),
-            pltpu.VMEM((wide, HEAD_DIM), low),
-            pltpu.VMEM((wide, HEAD_DIM), low),
-            pltpu.VMEM((HEAD_DIM, wide), full),
+            pltpu.VMEM((blocks, wide, HEAD_DIM), low),
+            pltpu.VMEM((blocks, wide, HEAD_DIM), low),
+            pltpu.VMEM((blocks, 1, wide), full),
+            pltpu.VMEM((blocks, 1, wide), full),
+            pltpu.VMEM((blocks, HEAD_DIM, wide), full),
             pltpu.VMEM((window, HEAD_DIM), full),
             pltpu.VMEM((window, HEAD_DIM), full),
             pltpu.VMEM((rows, width), low),
@@ -925,7 +978,7 @@
             dma((len(plan), 2)),
         ],
         compiler_params=pltpu.CompilerParams(
-            collective_id=0, has_side_effects=True, vmem_limit_bytes=48 * 1024 * 1024
+            collective_id=0, has_side_effects=True, vmem_limit_bytes=56 * 1024 * 1024
         ),
         name="whole",
     )(queries, keys, values, grad_out, delta, doc_lengths[None])

time: 108 us -> 98.7 us (0.914)
  Pallas kernels: 105 us -> 94.5 us
    pallas_call x1, Pallas kernels: 103 us -> 93.4 us  [whole(): pl.pallas_call(functools.partial(whole_kernel, shards, plan), out_shape=(...]
where the time goes in v7:
time: 98.7 us; the launch traced here: 98.4 us
  Pallas kernels  94.5 us (96%)
  other arithmetic  2.14 us (2%)
  between operations  1.47 us (1%)
    pallas_call x1, Pallas kernels, whole(): pl.pallas_call(functools.partial(whole_kernel, shards, plan), out_shape=(...  93.4 us

profile of v7, /device:TPU:8, one launch (start us, length us, event | category | flops | bytes accessed | tf_op | source)
XLA Modules:
  0.0 98.4 jit_solution(13350849918254840034)
XLA Ops:
  0.6 0.8 select_reduce_fusion.1
  1.4 1.3 %compare_reduce_fusion = pred[]{:T(512)} fusion(s32[256]{0:T(256)S(1)} %select_reduce_fusion.1, s32[256]{0:T(256)} %param.13), kind=kLoop, calls=%fused_computation.7 | loop fusion | flops 13823 | bytes 2049 | tf_op jit(solution)/shard_map/reduce_and | solution.py:1023
  3.4 93.6 %conditional.1 = ((bf16[128,4096]{1,0:T(8,128)(2,1)S(1)}, bf16[128,1024]{1,0:T(8,128)(2,1)S(1)}, bf16[128,1024]{1,0:T(8,128)(2,1)S(1)})) conditional(s32[]{:T(128)} %convert_element_type.3, (s32[256]{0:T(256)S(1)}, bf16[128,4096]{1,0:T(8,128)(2,1)}, bf16[128,1024]{1,0:T(8,128)(2,1)}, bf16[128,1024]{1,0:T(8,128)(2,1)}, bf16[128,4096]{1,0:T(8,128)(2,1)}, ...), branch_computations={%region_2.4_spmd, %region_4.5_spmd} | conditional | flops 787461 | bytes 21608 | solution.py:1036
  3.4 93.4 %whole.1 = (bf16[128,4096]{1,0:T(8,128)(2,1)S(1)}, bf16[128,1024]{1,0:T(8,128)(2,1)S(1)}, bf16[128,1024]{1,0:T(8,128)(2,1)S(1)}) custom-call(bf16[128,4096]{1,0:T(8,128)(2,1)} %get-tuple-element.38.q_in, bf16[128,1024]{1,0:T(8,128)(2,1)} %get-tuple-element.39.k_in, bf16[128,1024]{1,0:T(8,128)(2,1)} %get-tuple-element.40.v_in, ...), custom_call_target="tpu_custom_call" | custom-call | tf_op jit(solution)/shard_map/cond/branch_1_fun/whole/pallas_call | solution.py:940
  97.0 1.2 %settle.1 = (bf16[128,4096]{1,0:T(8,128)(2,1)}, bf16[128,1024]{1,0:T(8,128)(2,1)}, bf16[128,1024]{1,0:T(8,128)(2,1)}) custom-call(bf16[128,4096]{1,0:T(8,128)(2,1)S(1)} %get-tuple-element.50.refs_0_, bf16[128,1024]{1,0:T(8,128)(2,1)S(1)} %get-tuple-element.51.refs_1_, bf16[128,1024]{1,0:T(8,128)(2,1)S(1)} %get-tuple-element.52.refs_2_), custom_call_target="tpu_custom_call" | custom-call | tf_op jit(solution)/shard_map/settle/pallas_call | solution.py:1000

commit v8 on v7

--- a/solution.py
+++ b/solution.py
@@ -43,7 +43,7 @@
 
 
 def short_reach(blocks, shards, rows):
-    shard = blocks // (rows // BLOCK)
+    shard = lax.shift_right_logical(blocks, jnp.int32((rows // BLOCK).bit_length() - 1))
     reach = jnp.where(shard == 0, 0, blocks * BLOCK - TILE)
     for first in long_firsts(shards):
         opening = first * rows + rows // 2
@@ -764,7 +764,6 @@
     for which in range(2):
         arrived(which)
         for_runs(lambda run, *_: halo_copy(run, which).start(), True)
-    begin(5, 6)
 
     reach_tiles = halo // TILE
     key_offset = lax.broadcasted_iota(jnp.int32, (STEP, BLOCK), 0)
@@ -883,6 +882,7 @@
 
     arrived(3)
     for_runs(lambda run, *_: halo_copy(run, 0).wait_recv(), False)
+    begin(5, 6)
     attend_sums(0)
     arrived(2, 4)
     for_runs(lambda run, *_: halo_copy(run, 1).wait_recv(), False)
@@ -1019,7 +1019,9 @@
             jnp.where(doc_starts[:, None] <= places[None, :], doc_starts[:, None], 0), axis=0
         )
 
-    last_block = lax.div(doc_starts + doc_lengths - 1, jnp.int32(BLOCK))
+    last_block = lax.shift_right_logical(
+        doc_starts + doc_lengths - 1, jnp.int32(BLOCK.bit_length() - 1)
+    )
     fits = jnp.all(doc_starts >= short_reach(last_block, shards, rows))
 
     def in_one(*operands):

time: 98.7 us -> 98.6 us (level)
  no operation moved by 1% of the time
where the time goes in v8:
time: 98.6 us; the launch traced here: 98.3 us
  Pallas kernels  94.5 us (96%)
  other arithmetic  2.13 us (2%)
  between operations  1.47 us (1%)
    pallas_call x1, Pallas kernels, whole(): pl.pallas_call(functools.partial(whole_kernel, shards, plan), out_shape=(...  93.3 us

profile of v8, /device:TPU:8, one launch (start us, length us, event | category | flops | bytes accessed | tf_op | source)
XLA Modules:
  0.0 98.3 jit_solution(18333037402517877092)
XLA Ops:
  0.6 0.8 select_reduce_fusion.1
  1.4 1.3 %compare_reduce_fusion = pred[]{:T(512)} fusion(s32[256]{0:T(256)S(1)} %select_reduce_fusion.1, s32[256]{0:T(256)} %param.13), kind=kLoop, calls=%fused_computation.5 | loop fusion | flops 8959 | bytes 2049 | tf_op jit(solution)/shard_map/reduce_and | solution.py:1025
  3.4 93.6 %conditional.1 = ((bf16[128,4096]{1,0:T(8,128)(2,1)S(1)}, bf16[128,1024]{1,0:T(8,128)(2,1)S(1)}, bf16[128,1024]{1,0:T(8,128)(2,1)S(1)})) conditional(s32[]{:T(128)} %convert_element_type.3, (s32[256]{0:T(256)S(1)}, bf16[128,4096]{1,0:T(8,128)(2,1)}, bf16[128,1024]{1,0:T(8,128)(2,1)}, bf16[128,1024]{1,0:T(8,128)(2,1)}, bf16[128,4096]{1,0:T(8,128)(2,1)}, ...), branch_computations={%region_2.4_spmd, %region_4.5_spmd} | conditional | flops 787461 | bytes 21608 | solution.py:1038
  3.4 93.3 %whole.1 = (bf16[128,4096]{1,0:T(8,128)(2,1)S(1)}, bf16[128,1024]{1,0:T(8,128)(2,1)S(1)}, bf16[128,1024]{1,0:T(8,128)(2,1)S(1)}) custom-call(bf16[128,4096]{1,0:T(8,128)(2,1)} %get-tuple-element.38.q_in, bf16[128,1024]{1,0:T(8,128)(2,1)} %get-tuple-element.39.k_in, bf16[128,1024]{1,0:T(8,128)(2,1)} %get-tuple-element.40.v_in, ...), custom_call_target="tpu_custom_call" | custom-call | tf_op jit(solution)/shard_map/cond/branch_1_fun/whole/pallas_call | solution.py:940
  97.0 1.2 %settle.1 = (bf16[128,4096]{1,0:T(8,128)(2,1)}, bf16[128,1024]{1,0:T(8,128)(2,1)}, bf16[128,1024]{1,0:T(8,128)(2,1)}) custom-call(bf16[128,4096]{1,0:T(8,128)(2,1)S(1)} %get-tuple-element.50.refs_0_, bf16[128,1024]{1,0:T(8,128)(2,1)S(1)} %get-tuple-element.51.refs_1_, bf16[128,1024]{1,0:T(8,128)(2,1)S(1)} %get-tuple-element.52.refs_2_), custom_call_target="tpu_custom_call" | custom-call | tf_op jit(solution)/shard_map/settle/pallas_call | solution.py:1000
